TPU v7x, 32 devices: a whole 2x2x4 slice. The times are simulated.
32 devices in a mesh: tile: 8 (over y, x, core), col: 4 (over z).
Axes of the slice: x: 2, y: 2, z: 4, core: 2. Of those that a mesh axis runs over, the one named last changes fastest.
Arguments:
- impedance: bfloat16 [2, 16384, 16384], P(None, 'tile', 'col'), may hold values from -0.0234375 to 0.0234375
- mobility: bfloat16 [256, 64, 128], P('tile'), may hold values from -0.5 to 0.5
- force: bfloat16 [512, 256, 128], P('col', 'tile'), may hold values from -6 to 6
- patch_map: int32 [16384], replicated, may hold values from 0 to 16383, each once
- ownership: int32 [256], P('tile'), may hold values from 0 to 255, each once
Outputs:
- velocity: bfloat16 [512, 256, 128], P('col', 'tile')
- pressure: bfloat16 [512, 2, 16384], P('col', None, 'tile')
Inputs may be any that keep to these rules, and one draw needn't show every extreme that they name: `patch_map`: each patch appears exactly once. `ownership`: each panel appears exactly once.
All inputs are finite; a program needn't handle non-finite values.
Results may differ from a plain program's by a relative error of at most 0.018.
Values may be sent and summed in bfloat16 or wider, within the bound.
A program may use at most 128 MiB of HBM per device.

v0:
```python
import functools

import jax
import jax.numpy as jnp
from jax import lax
from jax.experimental import pallas as pl
from jax.experimental.pallas import tpu as pltpu
from jax.sharding import PartitionSpec as P

ITERS = 2
LANES = 128
BF16 = jnp.bfloat16
F32 = jnp.float32


MESH = pl.DeviceIdType.MESH


def gather_over_tile(tiles, x_ref, buf, send_sem, recv_sem, own_sem, ready):
    a_size = tiles // 4
    rows = x_ref.shape[0]
    half = rows // 2
    me = lax.axis_index("tile")
    core = lax.rem(me, 2)
    my_b = lax.rem(me // 2, 2)
    my_a = me // 4
    others = range(1, a_size)

    def chip_at(oa, ob):
        return lax.rem(my_a + oa, a_size) * 2 + lax.rem(my_b + ob, 2)

    def device_at(oa, ob):
        return chip_at(oa, ob) * 2 + core

    partner = chip_at(0, 0) * 2 + 1 - core
    neighbours = [partner, device_at(0, 1)] + [device_at(o, 0) for o in others]

    barrier = pltpu.get_barrier_semaphore()
    for device in neighbours:
        pl.semaphore_signal(barrier, inc=1, device_id={"tile": device}, device_id_type=MESH)
    pl.semaphore_wait(barrier, len(neighbours))

    def piece(oa, ob, h, owner_core):
        return buf.at[chip_at(oa, ob), pl.ds(pl.multiple_of(owner_core * rows + h * half, half), half)]

    sent = []

    def send(src, dst, device, relayed, oa, ob, h):
        copy = pltpu.make_async_remote_copy(
            src_ref=src,
            dst_ref=dst,
            send_sem=send_sem.at[len(sent)],
            recv_sem=recv_sem.at[relayed, oa * 2 + ob, h],
            device_id={"tile": device},
            device_id_type=MESH,
        )
        copy.start()
        sent.append(copy)

    def arrived(relayed, oa, ob, h):
        slot = piece(oa, ob, h, 1 - core if relayed else core)
        pltpu.make_async_remote_copy(
            src_ref=slot,
            dst_ref=slot,
            send_sem=send_sem.at[0],
            recv_sem=recv_sem.at[relayed, oa * 2 + ob, h],
            device_id={"tile": partner},
            device_id_type=MESH,
        ).wait_recv()

    def relay(oa, ob, h):
        slot = piece(oa, ob, h, core)
        send(slot, slot, partner, 1, oa, ob, h)

    def forward(oa, ob, h, device, new_oa, new_ob):
        slot = piece(oa, ob, h, core)
        send(slot, slot, device, 0, new_oa, new_ob, h)

    def own(h):
        return x_ref.at[pl.ds(h * half, half)]

    for h in (1, 0):
        send(own(h), piece(0, 0, h, core), device_at(0, 1), 0, 0, 1, h)
    for h in (0, 1):
        for o in others:
            send(own(h), piece(0, 0, h, core), device_at(o, 0), 0, (a_size - o) % a_size, 0, h)
    for h in (0, 1):
        send(own(h), piece(0, 0, h, core), partner, 1, 0, 0, h)
    local = pltpu.make_async_copy(
        x_ref, buf.at[chip_at(0, 0), pl.ds(pl.multiple_of(core * rows, rows), rows)], own_sem.at[0]
    )
    local.start()
    local.wait()
    for h in (0, 1):
        arrived(1, 0, 0, h)
    ready(chip_at(0, 0))

    arrived(0, 0, 1, 1)
    for o in others:
        forward(0, 1, 1, device_at(o, 0), (a_size - o) % a_size, 1)
    for o in others:
        arrived(0, o, 0, 0)
        forward(o, 0, 0, device_at(0, 1), o, 1)
    relay(0, 1, 1)
    for o in others:
        relay(o, 0, 0)
    arrived(0, 0, 1, 0)
    relay(0, 1, 0)
    for o in others:
        arrived(0, o, 0, 1)
        relay(o, 0, 1)
    for h in (1, 0):
        arrived(1, 0, 1, h)
    ready(chip_at(0, 1))
    for o in others:
        for h in (0, 1):
            arrived(0, o, 1, h)
            relay(o, 1, h)
    for o in others:
        for h in (0, 1):
            arrived(1, o, 0, h)
        ready(chip_at(o, 0))
    for o in others:
        for h in (0, 1):
            arrived(1, o, 1, h)
        ready(chip_at(o, 1))
    for copy in sent:
        copy.wait_send()


def chip_order(tiles):
    a_size = tiles // 4
    me = lax.axis_index("tile")
    my_b = lax.rem(me // 2, 2)
    my_a = me // 4
    order = [(0, 0), (0, 1)] + [(o, b) for b in (0, 1) for o in range(1, a_size)]
    return [lax.rem(my_a + oa, a_size) * 2 + lax.rem(my_b + ob, 2) for oa, ob in order]


def gather_scratch(tiles, shape):
    a_size = tiles // 4
    copies = 2 + 2 * (a_size - 1) + 2 * (a_size - 1) + 2 * 2 * a_size
    return [
        pltpu.VMEM((tiles // 2, 2 * shape[0]) + shape[1:], BF16),
        pltpu.SemaphoreType.DMA((copies,)),
        pltpu.SemaphoreType.DMA((2, 2 * a_size, 2)),
        pltpu.SemaphoreType.DMA((1,)),
    ]


def pick_kernel(tiles, index_ref, x_ref, out_ref, buf, send_sem, recv_sem, own_sem):
    gather_over_tile(tiles, x_ref, buf, send_sem, recv_sem, own_sem, lambda chip: None)
    count = out_ref.shape[0]
    pair = buf.shape[1]
    step = 16

    @pl.loop(0, count // step)
    def _(block):
        base = block * step
        for k in range(step):
            index = index_ref[base + k]
            out_ref[base + k] = buf[index // pair, lax.rem(index, pair)]


def gather_and_pick(index, rows, tiles):
    return pl.pallas_call(
        functools.partial(pick_kernel, tiles),
        out_shape=jax.ShapeDtypeStruct((index.shape[0],) + rows.shape[1:], rows.dtype),
        in_specs=[
            pl.BlockSpec(memory_space=pltpu.SMEM),
            pl.BlockSpec(memory_space=pltpu.VMEM),
        ],
        out_specs=pl.BlockSpec(memory_space=pltpu.VMEM),
        scratch_shapes=gather_scratch(tiles, rows.shape),
        compiler_params=pltpu.CompilerParams(
            collective_id=0, has_side_effects=True, vmem_limit_bytes=40 * 2**20
        ),
    )(index, rows)


def product_kernel(tiles, z_ref, x_ref, out_ref, z_buf, z_sem, total, buf, send_sem, recv_sem, own_sem):
    groups, rows, width = out_ref.shape
    half = width // 2
    depth = z_buf.shape[3]
    block = min(256, rows)
    chips = chip_order(tiles)
    steps = len(chips)

    def fetch(step):
        start = pl.multiple_of(chips[step] * depth, depth)
        return pltpu.make_async_copy(z_ref.at[:, :, pl.ds(start, depth)], z_buf.at[step % 2], z_sem.at[step % 2])

    for step in range(min(2, steps)):
        fetch(step).start()
    done = []

    def ready(chip):
        step = len(done)
        done.append(step)
        fetch(step).wait()

        @pl.loop(0, rows // block)
        def _(i):
            at = pl.ds(pl.multiple_of(i * block, block), block)
            x = buf[chip]
            a = jnp.dot(z_buf[step % 2, 0, at, :], x, preferred_element_type=F32)
            b = jnp.dot(z_buf[step % 2, 1, at, :], x, preferred_element_type=F32)
            for g in range(groups):
                re = slice(g * width, g * width + half)
                im = slice(g * width + half, (g + 1) * width)
                term = jnp.concatenate([a[:, re] - b[:, im], a[:, im] + b[:, re]], 1)
                if step > 0:
                    term = total[g, at, :] + term
                if step < steps - 1:
                    total[g, at, :] = term
                else:
                    out_ref[g, at, :] = term.astype(out_ref.dtype)

        if step + 2 < steps:
            fetch(step + 2).start()

    gather_over_tile(tiles, x_ref, buf, send_sem, recv_sem, own_sem, ready)


def gather_and_multiply(impedance, x, groups, tiles):
    _, rows, depth = impedance.shape
    width = x.shape[1] // groups
    return pl.pallas_call(
        functools.partial(product_kernel, tiles),
        out_shape=jax.ShapeDtypeStruct((groups, rows, width), BF16),
        in_specs=[
            pl.BlockSpec(memory_space=pl.ANY),
            pl.BlockSpec(memory_space=pltpu.VMEM),
        ],
        out_specs=pl.BlockSpec(memory_space=pltpu.VMEM),
        scratch_shapes=[
            pltpu.VMEM((2, 2, rows, 2 * x.shape[0]), BF16),
            pltpu.SemaphoreType.DMA((2,)),
            pltpu.VMEM((groups, rows, width), F32),
        ]
        + gather_scratch(tiles, x.shape),
        compiler_params=pltpu.CompilerParams(
            collective_id=1, has_side_effects=True, vmem_limit_bytes=60 * 2**20
        ),
    )(impedance, x)


def inverse_permutation(sigma):
    count = sigma.shape[0]
    where = jnp.arange(count, dtype=jnp.int32)
    high = (sigma // LANES)[None, :] == jnp.arange(count // LANES, dtype=jnp.int32)[:, None]
    low = (sigma % LANES)[:, None] == jnp.arange(LANES, dtype=jnp.int32)[None, :]
    where_high = jnp.where(low, (where // LANES)[:, None], 0).astype(BF16)
    where_low = jnp.where(low, (where % LANES)[:, None], 0).astype(BF16)
    digits = jnp.dot(
        high.astype(BF16), jnp.concatenate([where_high, where_low], 1), preferred_element_type=F32
    )
    inverse = digits[:, :LANES] * LANES + digits[:, LANES:]
    return inverse.astype(jnp.int32).reshape(count)


def per_device(impedance, mobility, force, patch_map, ownership):
    slots, width, _ = mobility.shape
    patches = patch_map.shape[0]
    loads = force.shape[0]
    tiles = lax.axis_size("tile")
    cols = lax.axis_size("col")
    share = patches // cols // tiles
    mine = slots * width
    tile = lax.axis_index("tile")

    panels = patch_map.reshape(-1, width)
    slot_flat = panels[ownership].reshape(mine)
    owners = lax.all_gather(ownership, "tile", axis=0, tiled=True)
    inverse = inverse_permutation(panels[owners].reshape(patches))
    share_index = lax.dynamic_index_in_dim(
        inverse.reshape(cols, tiles, share), tile, 1, keepdims=False
    ).reshape(cols * share)

    mob_re = mobility[:, :, :width]
    mob_im = mobility[:, :, width:]
    form = jnp.stack(
        [jnp.stack([mob_re, -mob_im], -1), jnp.stack([mob_im, mob_re], -1)], 2
    ).reshape(slots, 2 * width, 2 * width)
    force_rows = force.reshape(loads, slots, 2, width).transpose(1, 3, 2, 0).reshape(slots, 2 * width, loads)

    def response(drive):
        return lax.dot_general(
            form, drive, (((2,), (1,)), ((0,), (0,))), preferred_element_type=F32
        ).astype(BF16)

    velocity = response(force_rows)
    for _ in range(ITERS):
        picked = gather_and_pick(share_index, velocity.reshape(mine, 2, loads), tiles)
        picked = picked.reshape(cols, share, 2, loads)
        moved = lax.all_to_all(picked, "col", split_axis=0, concat_axis=0, tiled=True)
        columns = moved.transpose(1, 0, 2, 3).reshape(share, cols * 2 * loads)
        partial = gather_and_multiply(impedance, columns, cols, tiles)
        summed = lax.psum_scatter(partial, "col", scatter_dimension=0, tiled=True)
        pressure = summed.reshape(-1, 2, loads)
        at_slots = gather_and_pick(slot_flat, pressure, tiles).reshape(slots, 2 * width, loads)
        drive = (force_rows.astype(F32) - at_slots.astype(F32)).astype(BF16)
        velocity = response(drive)
    velocity_out = velocity.reshape(slots, width, 2, loads).transpose(3, 0, 2, 1).reshape(loads, slots, 2 * width)
    pressure_out = pressure.transpose(2, 1, 0)
    return velocity_out, pressure_out


def solution(mesh):
    return jax.shard_map(
        per_device,
        mesh=mesh,
        in_specs=(
            P(None, "tile", "col"),
            P("tile", None, None),
            P("col", "tile", None),
            P(),
            P("tile"),
        ),
        out_specs=(P("col", "tile", None), P("col", None, "tile")),
        check_vma=False,
    )
```

profile of v0, /device:TPU:0, one launch (start us, length us, event | category | flops | bytes accessed | tf_op | source)
XLA Modules:
  0.0 611.9 jit_solution(12387033931931515888)
XLA Ops:
  7.2 0.9 reshape.136
  8.2 1.2 dynamic-slice
  10.1 0.9 dynamic-update-slice
  10.9 9.5 %all-reduce = s32[256]{0:T(256)S(1)} all-reduce(s32[256]{0:T(256)S(1)} %dynamic-update-slice), channel_id=1, replica_groups=mesh['tile'=8,'col'=4] {'tile'}, use_global_device_ids=true, to_apply=%add | all-reduce | flops 256 | bytes 2048
  20.4 0.7 gather_fusion.1
  21.3 7.8 %select_convert_fusion.1 = (bf16[16384,128]{1,0:T(8,128)(2,1)S(1)}, bf16[16384,128]{1,0:T(8,128)(2,1)S(1)}) fusion(s32[16384]{0:T(1024)S(1)} %get-tuple-element.20, s32[16384]{0:T(1024)S(1)} %get-tuple-element.16, s32[16384]{0:T(1024)S(1)} %get-tuple-element.19), kind=kLoop, calls=%fused_computation.7 | loop fusion | flops 10485760 | bytes 8585216 | tf_op jit(solution)/shard_map/convert_element_type | solution.py:253
  29.1 1.3 fusion
  31.7 7.7 %copy.39 = bf16[32,64,2,64,2]{0,4,3,2,1:T(2,128)(2,1)} copy(bf16[32,64,2,64,2]{3,1,0,4,2:T(8,128)(2,1)S(1)} %pad_maximum_fusion) | data formatting | bytes 2097152 | tf_op jit(solution)/shard_map/stack | solution.py:282
  39.4 4.1 copy.50
  43.5 1.0 copy.40
  45.2 0.8 convolution_convert_fusion.2
  45.9 51.1 %shard_map.68 = bf16[2048,2,128]{2,1,0:T(2,128)(2,1)S(1)} custom-call(s32[2048]{0:T(1024)S(1)} %bitcast.48, bf16[2048,2,128]{2,1,0:T(2,128)(2,1)S(1)} %bitcast.45), custom_call_target="tpu_custom_call" | custom-call | tf_op jit(solution)/shard_map/pallas_call | solution.py:166
  97.1 31.0 %all_to_all.10 = bf16[4,512,2,128]{3,2,1,0:T(2,128)(2,1)S(1)} all-to-all(bf16[4,512,2,128]{3,2,1,0:T(2,128)(2,1)S(1)} %bitcast.47), channel_id=1, replica_groups=mesh['tile'=8,'col'=4] {'col'}, dimensions={0} | all-to-all | bytes 2097152 | tf_op jit(solution)/shard_map/all_to_all | solution.py:296
  128.1 0.7 copy.44
  128.8 1.5 reshape.142.x_ref
  130.4 59.9 %shard_map.69 = bf16[4,2048,256]{2,1,0:T(8,128)(2,1)} custom-call(bf16[2,2048,4096]{2,1,0:T(8,128)(2,1)} %z_ref.3, bf16[512,1024]{1,0:T(8,128)(2,1)} %reshape.142.x_ref), custom_call_target="tpu_custom_call" | custom-call | tf_op jit(solution)/shard_map/pallas_call | solution.py:228
  191.5 75.3 %reduce-scatter.3.cloned.1.call-done = bf16[1,2048,256]{2,1,0:T(8,128)(2,1)} async-done(((bf16[4,2048,256]{2,1,0:T(8,128)(2,1)}), bf16[1,2048,256]{2,1,0:T(8,128)(2,1)}) %reduce-scatter.3.cloned.1.call-update) | async-done | bytes 1048592 | tf_op jit(solution)/shard_map/reduce_scatter | solution.py:299
  266.8 1.3 reshape.143.x_ref
  268.1 52.0 %shard_map.70 = bf16[2048,2,128]{2,1,0:T(2,128)(2,1)S(1)} custom-call(s32[2048]{0:T(1024)S(1)} %reshape.137.index_ref, bf16[2048,2,128]{2,1,0:T(2,128)(2,1)S(1)} %reshape.143.x_ref), custom_call_target="tpu_custom_call" | custom-call | tf_op jit(solution)/shard_map/pallas_call | solution.py:166
  320.4 1.4 fusion.5
  321.7 0.7 convolution_convert_fusion.1
  322.5 52.0 %shard_map.71 = bf16[2048,2,128]{2,1,0:T(2,128)(2,1)S(1)} custom-call(s32[2048]{0:T(1024)S(1)} %bitcast.49, bf16[2048,2,128]{2,1,0:T(2,128)(2,1)S(1)} %bitcast.42), custom_call_target="tpu_custom_call" | custom-call | tf_op jit(solution)/shard_map/pallas_call | solution.py:166
  374.5 30.6 %all_to_all.11 = bf16[4,512,2,128]{3,2,1,0:T(2,128)(2,1)S(1)} all-to-all(bf16[4,512,2,128]{3,2,1,0:T(2,128)(2,1)S(1)} %bitcast.46), channel_id=1, replica_groups=mesh['tile'=8,'col'=4] {'col'}, dimensions={0} | all-to-all | bytes 2097152 | tf_op jit(solution)/shard_map/all_to_all | solution.py:296
  405.8 1.5 reshape.146.x_ref
  407.3 59.8 %shard_map.72 = bf16[4,2048,256]{2,1,0:T(8,128)(2,1)} custom-call(bf16[2,2048,4096]{2,1,0:T(8,128)(2,1)} %z_ref.3, bf16[512,1024]{1,0:T(8,128)(2,1)} %reshape.146.x_ref), custom_call_target="tpu_custom_call" | custom-call | tf_op jit(solution)/shard_map/pallas_call | solution.py:228
  467.1 76.6 %reduce-scatter.5.cloned.1.call-done = bf16[1,2048,256]{2,1,0:T(8,128)(2,1)} async-done(((bf16[4,2048,256]{2,1,0:T(8,128)(2,1)}), bf16[1,2048,256]{2,1,0:T(8,128)(2,1)}) %reduce-scatter.5.cloned.1.call-update) | async-done | bytes 1048592 | tf_op jit(solution)/shard_map/reduce_scatter | solution.py:299
  543.7 1.3 reshape.147.x_ref
  545.1 52.0 %shard_map.73 = bf16[2048,2,128]{2,1,0:T(2,128)(2,1)S(1)} custom-call(s32[2048]{0:T(1024)S(1)} %reshape.137.index_ref, bf16[2048,2,128]{2,1,0:T(2,128)(2,1)S(1)} %reshape.147.x_ref), custom_call_target="tpu_custom_call" | custom-call | tf_op jit(solution)/shard_map/pallas_call | solution.py:166
  597.3 1.4 fusion.6
  598.7 0.7 convolution_convert_fusion
  599.7 1.7 copy.53
  601.4 3.7 copy.54
  (31 shorter events, 4.9 us)
Async XLA Ops:
  7.2 259.6 %reduce-scatter.3.cloned.1.call-start = ((), (), s32[]{:S(2)}) async-start(), calls=%async_computation.4 | async-start | bytes 5242880 | tf_op jit(solution)/shard_map/reduce_scatter | solution.py:299
  29.1 1.3 copy-start
  39.4 4.1 copy-start.1
  190.2 0.7 copy-start.2
  190.3 353.5 %reduce-scatter.5.cloned.1.call-start = ((), (), s32[]{:S(2)}) async-start(), calls=%async_computation.5 | async-start | bytes 5242880 | tf_op jit(solution)/shard_map/reduce_scatter | solution.py:299
Sparse Core Ops, SparseCore 0:
  190.4 76.3 reduce-scatter.2
  467.2 76.4 reduce-scatter.4
where the time goes:
time: 612 us
  Pallas kernels  327 us (53%)
  waiting for transfers between devices  152 us (25%)
  blocking collectives  71.1 us (12%)
  local copies, waits for them, and re-layouts  31.2 us (5%)
  between operations  15 us (2%)
  other arithmetic  12.3 us (2%)
    pallas_call x4, Pallas kernels, gather_and_pick(): pl.pallas_call(functools.partial(pick_kernel, tiles), out_shape=jax.Shape...  207 us
    reduce_scatter x2, waiting for transfers between devices, per_device(): summed = lax.psum_scatter(partial, 'col', scatter_dimension=0, tiled=True)  152 us
    pallas_call x2, Pallas kernels, gather_and_multiply(): pl.pallas_call(functools.partial(product_kernel, tiles), out_shape=jax.Sh...  120 us
    all_to_all x2, blocking collectives, per_device(): lax.all_to_all(picked, 'col', split_axis=0, concat_axis=0, tiled=True)  61.6 us
  transfers between devices with their start and end apart: 2, of which 2 were waited for; matrix products, arithmetic and copies ran while one was open for 0% of the time, Pallas kernels for 0%

commit v1 on v0

--- a/solution.py
+++ b/solution.py
@@ -126,15 +126,6 @@
         ready(chip_at(o, 1))
     for copy in sent:
         copy.wait_send()
-
-
-def chip_order(tiles):
-    a_size = tiles // 4
-    me = lax.axis_index("tile")
-    my_b = lax.rem(me // 2, 2)
-    my_a = me // 4
-    order = [(0, 0), (0, 1)] + [(o, b) for b in (0, 1) for o in range(1, a_size)]
-    return [lax.rem(my_a + oa, a_size) * 2 + lax.rem(my_b + ob, 2) for oa, ob in order]
 
 
 def gather_scratch(tiles, shape):
@@ -178,67 +169,330 @@
     )(index, rows)
 
 
-def product_kernel(tiles, z_ref, x_ref, out_ref, z_buf, z_sem, total, buf, send_sem, recv_sem, own_sem):
-    groups, rows, width = out_ref.shape
-    half = width // 2
-    depth = z_buf.shape[3]
+def couple_kernel(
+    tiles,
+    cols,
+    block,
+    z_ref,
+    x_ref,
+    out_ref,
+    z_buf,
+    z_sem,
+    buf,
+    part,
+    sums,
+    swap_send,
+    swap_recv,
+    own_sem,
+    send_sem,
+    recv_sem,
+    sum_send,
+    sum_recv,
+):
+    a_size = tiles // 4
+    rows, width = out_ref.shape
+    share = x_ref.shape[1]
+    half = share // 2
+    lanes = width // 2
+    blocks = rows // block
+    col = lax.axis_index("col")
+    me = lax.axis_index("tile")
+    core = lax.rem(me, 2)
+    my_b = lax.rem(me // 2, 2)
+    my_a = me // 4
+    others = range(1, a_size)
+
+    def chip_at(oa, ob):
+        return lax.rem(my_a + oa, a_size) * 2 + lax.rem(my_b + ob, 2)
+
+    def device_at(oa, ob):
+        return chip_at(oa, ob) * 2 + core
+
+    partner = chip_at(0, 0) * 2 + 1 - core
+    neighbours = [partner, device_at(0, 1)] + [device_at(o, 0) for o in others]
+
+    barrier = pltpu.get_barrier_semaphore()
+    for device in neighbours:
+        pl.semaphore_signal(barrier, inc=1, device_id={"tile": device}, device_id_type=MESH)
+    for o in range(1, cols):
+        pl.semaphore_signal(barrier, inc=1, device_id={"col": lax.rem(col + o, cols)}, device_id_type=MESH)
+
+    def at(i):
+        return pl.ds(pl.multiple_of(i * block, block), block)
+
+    def fetch(i):
+        return pltpu.make_async_copy(z_ref.at[:, at(i)], z_buf.at[:, at(i)], z_sem.at[i])
+
+    @pl.loop(0, blocks)
+    def _(i):
+        fetch(i).start()
+
+    near = jnp.minimum(col, cols - 1 - col)
+
+    def group(k):
+        side = col + (k + 1) // 2 if k % 2 else col - k // 2
+        rest = jnp.where(near == col, k, cols - 1 - k)
+        return jnp.where(k <= 2 * near, side, rest)
+
+    order = [col] + [group(k) for k in range(1, cols)]
+
+    def piece(g, oa, ob, h, owner_core):
+        start = (chip_at(oa, ob) * 2 + owner_core) * share + h * half
+        return buf.at[g, pl.ds(pl.multiple_of(start, half), half)]
+
+    own_rows = pl.ds(pl.multiple_of(me * share, share), share)
+
+    pl.semaphore_wait(barrier, len(neighbours) + cols - 1)
+
+    def swap(k):
+        return pltpu.make_async_remote_copy(
+            src_ref=x_ref.at[order[k]],
+            dst_ref=buf.at[col, own_rows],
+            send_sem=swap_send.at[k - 1],
+            recv_sem=swap_recv.at[col],
+            device_id={"col": order[k]},
+            device_id_type=MESH,
+        )
+
+    for k in range(1, cols):
+        swap(k).start()
+
+    sent = []
+
+    def gather(k):
+        g = order[k]
+
+        def send(src, dst, device, relayed, oa, ob, h):
+            copy = pltpu.make_async_remote_copy(
+                src_ref=src,
+                dst_ref=dst,
+                send_sem=send_sem.at[len(sent)],
+                recv_sem=recv_sem.at[k, relayed, oa * 2 + ob, h],
+                device_id={"tile": device},
+                device_id_type=MESH,
+            )
+            copy.start()
+            sent.append(copy)
+
+        def arrived(relayed, oa, ob, h):
+            slot = piece(g, oa, ob, h, 1 - core if relayed else core)
+            pltpu.make_async_remote_copy(
+                src_ref=slot,
+                dst_ref=slot,
+                send_sem=send_sem.at[0],
+                recv_sem=recv_sem.at[k, relayed, oa * 2 + ob, h],
+                device_id={"tile": partner},
+                device_id_type=MESH,
+            ).wait_recv()
+
+        def relay(oa, ob, h):
+            slot = piece(g, oa, ob, h, core)
+            send(slot, slot, partner, 1, oa, ob, h)
+
+        def forward(oa, ob, h, device, new_oa, new_ob):
+            slot = piece(g, oa, ob, h, core)
+            send(slot, slot, device, 0, new_oa, new_ob, h)
+
+        if k == 0:
+            local = pltpu.make_async_copy(x_ref.at[g], buf.at[g, own_rows], own_sem.at[0])
+            local.start()
+            local.wait()
+        else:
+            slot = buf.at[g, own_rows]
+            pltpu.make_async_remote_copy(
+                src_ref=slot,
+                dst_ref=slot,
+                send_sem=swap_send.at[0],
+                recv_sem=swap_recv.at[g],
+                device_id={"col": g},
+                device_id_type=MESH,
+            ).wait_recv()
+        for h in (1, 0):
+            forward(0, 0, h, device_at(0, 1), 0, 1)
+        for h in (0, 1):
+            for o in others:
+                forward(0, 0, h, device_at(o, 0), (a_size - o) % a_size, 0)
+        for h in (0, 1):
+            relay(0, 0, h)
+        yield
+        arrived(0, 0, 1, 1)
+        for o in others:
+            forward(0, 1, 1, device_at(o, 0), (a_size - o) % a_size, 1)
+        for o in others:
+            arrived(0, o, 0, 0)
+            forward(o, 0, 0, device_at(0, 1), o, 1)
+        relay(0, 1, 1)
+        for o in others:
+            relay(o, 0, 0)
+        yield
+        arrived(0, 0, 1, 0)
+        relay(0, 1, 0)
+        for o in others:
+            arrived(0, o, 0, 1)
+            relay(o, 0, 1)
+        for h in (0, 1):
+            for o in others:
+                arrived(0, o, 1, h)
+                relay(o, 1, h)
+        for h in (0, 1):
+            arrived(1, 0, 0, h)
+        for h in (1, 0):
+            arrived(1, 0, 1, h)
+        for o in others:
+            for h in (0, 1):
+                arrived(1, o, 0, h)
+        for o in others:
+            for h in (0, 1):
+                arrived(1, o, 1, h)
+        yield
+
+    last = cols - 1
+    edge = jnp.logical_or(col == 0, col == last)
+
+    def pass_on(g, i):
+        below = jnp.logical_and(g < col, g == col - 1)
+        slot = jnp.where(below, cols, g)
+        return pltpu.make_async_remote_copy(
+            src_ref=sums.at[g, at(i)],
+            dst_ref=sums.at[slot, at(i)],
+            send_sem=sum_send.at[g, i],
+            recv_sem=sum_recv.at[slot, i],
+            device_id={"col": jnp.where(g > col, col + 1, col - 1)},
+            device_id_type=MESH,
+        )
+
+    def passed(slot, i):
+        pltpu.make_async_remote_copy(
+            src_ref=sums.at[slot, at(i)],
+            dst_ref=sums.at[slot, at(i)],
+            send_sem=sum_send.at[0, 0],
+            recv_sem=sum_recv.at[slot, i],
+            device_id={"col": lax.rem(col + 1, cols)},
+            device_id_type=MESH,
+        ).wait_recv()
+
+    def multiply(k, low, high):
+        g = order[k]
+
+        @pl.loop(low, high)
+        def _(i):
+            if k == 0:
+                fetch(i).wait()
+            x = buf[g]
+            a = jnp.dot(z_buf[0, at(i), :], x, preferred_element_type=F32)
+            b = jnp.dot(z_buf[1, at(i), :], x, preferred_element_type=F32)
+            term = jnp.concatenate([a[:, :lanes] - b[:, lanes:], a[:, lanes:] + b[:, :lanes]], 1)
+            if k == 0:
+                part[g, at(i), :] = term
+            else:
+
+                @pl.when(edge)
+                def _():
+                    sums[g, at(i), :] = term.astype(BF16)
+                    pass_on(g, i).start()
+
+                @pl.when(jnp.logical_not(edge))
+                def _():
+                    part[g, at(i), :] = term
+
+    stages = [gather(k) for k in range(cols)]
+    middle = blocks // 2
+    next(stages[0])
+    next(stages[0])
+    if cols > 1:
+        next(stages[1])
+    next(stages[0])
+    for k in range(cols):
+        multiply(k, 0, middle)
+        if k + 1 < cols:
+            next(stages[k + 1])
+        if k + 2 < cols:
+            next(stages[k + 2])
+        multiply(k, middle, blocks)
+        if k + 1 < cols:
+            next(stages[k + 1])
+
+    lag = min(2, blocks)
+    rising = 2 * col < cols
+
+    def flow(up, turn, i):
+        g = jnp.where(up, turn, last - turn)
+        due = jnp.where(up, g - col, col - g) > 0
+
+        @pl.when(due)
+        def _():
+            passed(g, i)
+            sums[g, at(i), :] = (sums[g, at(i), :].astype(F32) + part[g, at(i), :]).astype(BF16)
+            pass_on(g, i).start()
+
+    @pl.when(jnp.logical_not(edge))
+    def _():
+        for turn in range(1, cols):
+
+            @pl.loop(0, blocks + lag)
+            def _(i):
+                @pl.when(i < blocks)
+                def _():
+                    flow(rising, turn, i)
+
+                @pl.when(i >= lag)
+                def _():
+                    flow(jnp.logical_not(rising), turn, i - lag)
+
+    @pl.loop(0, blocks)
+    def _(i):
+        @pl.when(col > 0)
+        def _():
+            passed(col, i)
+            part[col, at(i), :] += sums[col, at(i), :].astype(F32)
+
+        @pl.when(col < last)
+        def _():
+            passed(cols, i)
+            part[col, at(i), :] += sums[cols, at(i), :].astype(F32)
+
+        out_ref[at(i), :] = part[col, at(i), :].astype(BF16)
+
+    for k in range(1, cols):
+
+        @pl.loop(0, blocks)
+        def _(i):
+            pass_on(order[k], i).wait_send()
+
+    for k in range(1, cols):
+        swap(k).wait_send()
+    for copy in sent:
+        copy.wait_send()
+
+
+def couple(impedance, x, tiles):
+    _, rows, depth = impedance.shape
+    cols, share, width = x.shape
+    a_size = tiles // 4
     block = min(256, rows)
-    chips = chip_order(tiles)
-    steps = len(chips)
-
-    def fetch(step):
-        start = pl.multiple_of(chips[step] * depth, depth)
-        return pltpu.make_async_copy(z_ref.at[:, :, pl.ds(start, depth)], z_buf.at[step % 2], z_sem.at[step % 2])
-
-    for step in range(min(2, steps)):
-        fetch(step).start()
-    done = []
-
-    def ready(chip):
-        step = len(done)
-        done.append(step)
-        fetch(step).wait()
-
-        @pl.loop(0, rows // block)
-        def _(i):
-            at = pl.ds(pl.multiple_of(i * block, block), block)
-            x = buf[chip]
-            a = jnp.dot(z_buf[step % 2, 0, at, :], x, preferred_element_type=F32)
-            b = jnp.dot(z_buf[step % 2, 1, at, :], x, preferred_element_type=F32)
-            for g in range(groups):
-                re = slice(g * width, g * width + half)
-                im = slice(g * width + half, (g + 1) * width)
-                term = jnp.concatenate([a[:, re] - b[:, im], a[:, im] + b[:, re]], 1)
-                if step > 0:
-                    term = total[g, at, :] + term
-                if step < steps - 1:
-                    total[g, at, :] = term
-                else:
-                    out_ref[g, at, :] = term.astype(out_ref.dtype)
-
-        if step + 2 < steps:
-            fetch(step + 2).start()
-
-    gather_over_tile(tiles, x_ref, buf, send_sem, recv_sem, own_sem, ready)
-
-
-def gather_and_multiply(impedance, x, groups, tiles):
-    _, rows, depth = impedance.shape
-    width = x.shape[1] // groups
+    copies = cols * (2 + 2 * (a_size - 1) + 2 * (a_size - 1) + 2 * 2 * a_size)
     return pl.pallas_call(
-        functools.partial(product_kernel, tiles),
-        out_shape=jax.ShapeDtypeStruct((groups, rows, width), BF16),
+        functools.partial(couple_kernel, tiles, cols, block),
+        out_shape=jax.ShapeDtypeStruct((rows, width), BF16),
         in_specs=[
             pl.BlockSpec(memory_space=pl.ANY),
             pl.BlockSpec(memory_space=pltpu.VMEM),
         ],
         out_specs=pl.BlockSpec(memory_space=pltpu.VMEM),
         scratch_shapes=[
-            pltpu.VMEM((2, 2, rows, 2 * x.shape[0]), BF16),
-            pltpu.SemaphoreType.DMA((2,)),
-            pltpu.VMEM((groups, rows, width), F32),
-        ]
-        + gather_scratch(tiles, x.shape),
+            pltpu.VMEM((2, rows, depth), BF16),
+            pltpu.SemaphoreType.DMA((rows // block,)),
+            pltpu.VMEM((cols, depth, width), BF16),
+            pltpu.VMEM((cols, rows, width), F32),
+            pltpu.VMEM((cols + 1, rows, width), BF16),
+            pltpu.SemaphoreType.DMA((max(cols - 1, 1),)),
+            pltpu.SemaphoreType.DMA((cols,)),
+            pltpu.SemaphoreType.DMA((1,)),
+            pltpu.SemaphoreType.DMA((copies,)),
+            pltpu.SemaphoreType.DMA((cols, 2, 2 * a_size, 2)),
+            pltpu.SemaphoreType.DMA((cols, rows // block)),
+            pltpu.SemaphoreType.DMA((cols + 1, rows // block)),
+        ],
         compiler_params=pltpu.CompilerParams(
             collective_id=1, has_side_effects=True, vmem_limit_bytes=60 * 2**20
         ),
@@ -292,11 +546,7 @@
     velocity = response(force_rows)
     for _ in range(ITERS):
         picked = gather_and_pick(share_index, velocity.reshape(mine, 2, loads), tiles)
-        picked = picked.reshape(cols, share, 2, loads)
-        moved = lax.all_to_all(picked, "col", split_axis=0, concat_axis=0, tiled=True)
-        columns = moved.transpose(1, 0, 2, 3).reshape(share, cols * 2 * loads)
-        partial = gather_and_multiply(impedance, columns, cols, tiles)
-        summed = lax.psum_scatter(partial, "col", scatter_dimension=0, tiled=True)
+        summed = couple(impedance, picked.reshape(cols, share, 2 * loads), tiles)
         pressure = summed.reshape(-1, 2, loads)
         at_slots = gather_and_pick(slot_flat, pressure, tiles).reshape(slots, 2 * width, loads)
         drive = (force_rows.astype(F32) - at_slots.astype(F32)).astype(BF16)

time: 612 us -> 508 us (0.83)
  waiting for transfers between devices: 152 us -> 0 us
  Pallas kernels: 327 us -> 451 us
  blocking collectives: 71.1 us -> 9.49 us
  between operations: 15 us -> 1.61 us
    reduce_scatter x2 -> x0, waiting for transfers between devices: 152 us -> none  [per_device(): summed = lax.psum_scatter(partial, 'col', scatter_dimension=0, tiled=True)]
    pallas_call x2, Pallas kernels: 120 us -> 245 us  [couple(): pl.pallas_call(functools.partial(couple_kernel, tiles, cols, block), out_...]
    all_to_all x2 -> x0, blocking collectives: 61.6 us -> none  [per_device(): lax.all_to_all(picked, 'col', split_axis=0, concat_axis=0, tiled=True)]
  transfers between devices with their start and end apart: 2 -> 0, of which waited for: 2 -> 0; matrix products, arithmetic and copies ran while one was open for 0% -> 0% of each run, Pallas kernels for 0% -> 0%
where the time goes in v1:
time: 508 us; the launch traced here: 507 us
  Pallas kernels  451 us (89%)
  local copies, waits for them, and re-layouts  29.4 us (6%)
  other arithmetic  12.3 us (2%)
  blocking collectives  9.49 us (2%)
    pallas_call x2, Pallas kernels, couple(): pl.pallas_call(functools.partial(couple_kernel, tiles, cols, block), out_...  245 us
    pallas_call x4, Pallas kernels, gather_and_pick(): pl.pallas_call(functools.partial(pick_kernel, tiles), out_shape=jax.Shape...  206 us

profile of v1, /device:TPU:0, one launch (start us, length us, event | category | flops | bytes accessed | tf_op | source)
XLA Modules:
  0.0 506.9 jit_solution(4826617819921846614)
XLA Ops:
  0.6 0.9 reshape.130
  1.6 1.2 dynamic-slice
  3.5 0.9 dynamic-update-slice
  4.3 9.5 %all-reduce = s32[256]{0:T(256)S(1)} all-reduce(s32[256]{0:T(256)S(1)} %dynamic-update-slice), channel_id=1, replica_groups=mesh['tile'=8,'col'=4] {'tile'}, use_global_device_ids=true, to_apply=%add | all-reduce | flops 256 | bytes 2048
  13.8 0.7 gather_fusion.1
  14.7 7.8 %select_convert_fusion.1 = (bf16[16384,128]{1,0:T(8,128)(2,1)S(1)}, bf16[16384,128]{1,0:T(8,128)(2,1)S(1)}) fusion(s32[16384]{0:T(1024)S(1)} %get-tuple-element.18, s32[16384]{0:T(1024)S(1)} %get-tuple-element.14, s32[16384]{0:T(1024)S(1)} %get-tuple-element.17), kind=kLoop, calls=%fused_computation.7 | loop fusion | flops 10485760 | bytes 8585216 | tf_op jit(solution)/shard_map/convert_element_type | solution.py:507
  22.6 1.3 fusion
  24.1 0.5 maximum_bitcast_fusion
  24.6 0.5 pad_maximum_fusion
  25.1 7.7 %copy.19 = bf16[32,64,2,64,2]{0,4,3,2,1:T(2,128)(2,1)} copy(bf16[32,64,2,64,2]{3,1,0,4,2:T(8,128)(2,1)S(1)} %pad_maximum_fusion) | data formatting | bytes 2097152 | tf_op jit(solution)/shard_map/stack | solution.py:536
  32.8 4.1 copy.28
  36.9 1.0 copy.20
  37.9 0.7 copy.21
  38.6 0.8 convolution_convert_fusion.2
  39.4 51.1 %shard_map.68 = bf16[2048,2,128]{2,1,0:T(2,128)(2,1)S(1)} custom-call(s32[2048]{0:T(1024)S(1)} %bitcast.42, bf16[2048,2,128]{2,1,0:T(2,128)(2,1)S(1)} %bitcast.41), custom_call_target="tpu_custom_call" | custom-call | tf_op jit(solution)/shard_map/pallas_call | solution.py:157
  90.5 1.5 reshape.135.x_ref
  92.0 121.6 %shard_map.69 = bf16[2048,256]{1,0:T(8,128)(2,1)} custom-call(bf16[2,2048,4096]{2,1,0:T(8,128)(2,1)} %z_ref.3, bf16[4,512,256]{2,1,0:T(8,128)(2,1)} %reshape.135.x_ref), custom_call_target="tpu_custom_call" | custom-call | tf_op jit(solution)/shard_map/pallas_call | solution.py:474
  213.6 1.3 reshape.136.x_ref
  215.0 0.6 gather_fusion
  215.6 51.4 %shard_map.70 = bf16[2048,2,128]{2,1,0:T(2,128)(2,1)S(1)} custom-call(s32[2048]{0:T(1024)S(1)} %reshape.131.index_ref, bf16[2048,2,128]{2,1,0:T(2,128)(2,1)S(1)} %reshape.136.x_ref), custom_call_target="tpu_custom_call" | custom-call | tf_op jit(solution)/shard_map/pallas_call | solution.py:157
  267.3 1.4 fusion.5
  268.7 0.8 convolution_convert_fusion.1
  269.4 52.0 %shard_map.71 = bf16[2048,2,128]{2,1,0:T(2,128)(2,1)S(1)} custom-call(s32[2048]{0:T(1024)S(1)} %bitcast.43, bf16[2048,2,128]{2,1,0:T(2,128)(2,1)S(1)} %bitcast.38), custom_call_target="tpu_custom_call" | custom-call | tf_op jit(solution)/shard_map/pallas_call | solution.py:157
  321.4 1.5 reshape.138.x_ref
  322.9 123.1 %shard_map.72 = bf16[2048,256]{1,0:T(8,128)(2,1)} custom-call(bf16[2,2048,4096]{2,1,0:T(8,128)(2,1)} %z_ref.3, bf16[4,512,256]{2,1,0:T(8,128)(2,1)} %reshape.138.x_ref), custom_call_target="tpu_custom_call" | custom-call | tf_op jit(solution)/shard_map/pallas_call | solution.py:474
  446.0 1.4 reshape.139.x_ref
  447.4 51.5 %shard_map.73 = bf16[2048,2,128]{2,1,0:T(2,128)(2,1)S(1)} custom-call(s32[2048]{0:T(1024)S(1)} %reshape.131.index_ref, bf16[2048,2,128]{2,1,0:T(2,128)(2,1)S(1)} %reshape.139.x_ref), custom_call_target="tpu_custom_call" | custom-call | tf_op jit(solution)/shard_map/pallas_call | solution.py:157
  499.2 1.4 fusion.6
  500.5 0.8 convolution_convert_fusion
  501.3 0.2 copy.30
  501.5 1.7 copy.31
  503.2 3.7 copy.32
  (25 shorter events, 1.0 us)
Async XLA Ops:
  22.5 1.3 copy-start.2
  32.8 4.1 copy-start.3
  38.6 228.7 %copy-start = (bf16[32,64,2,128]{3,0,2,1:T(8,128)(2,1)}, bf16[32,64,2,128]{3,0,2,1:T(8,128)(2,1)S(1)}, u32[]{:S(2)}) copy-start(bf16[32,64,2,128]{3,0,2,1:T(8,128)(2,1)S(1)} %copy.21) | copy-start | bytes 3145732
  92.0 122.9 %copy-start.4 = (s32[32]{0:T(128)S(1)}, s32[32]{0:T(128)}, u32[]{:S(2)}) copy-start(s32[32]{0:T(128)} %param.9) | copy-start | bytes 388
  446.0 53.2 %copy-start.1 = (bf16[32,64,2,128]{3,0,2,1:T(8,128)(2,1)S(1)}, bf16[32,64,2,128]{3,0,2,1:T(8,128)(2,1)}, u32[]{:S(2)}) copy-start(bf16[32,64,2,128]{3,0,2,1:T(8,128)(2,1)} %copy-done) | copy-start | bytes 3145732

commit v2 on v1

--- a/solution.py
+++ b/solution.py
@@ -16,7 +16,7 @@
 MESH = pl.DeviceIdType.MESH
 
 
-def gather_over_tile(tiles, x_ref, buf, send_sem, recv_sem, own_sem, ready):
+def gather_over_tile(tiles, x_ref, buf, send_sem, recv_sem, own_sem):
     a_size = tiles // 4
     rows = x_ref.shape[0]
     half = rows // 2
@@ -41,7 +41,8 @@
     pl.semaphore_wait(barrier, len(neighbours))
 
     def piece(oa, ob, h, owner_core):
-        return buf.at[chip_at(oa, ob), pl.ds(pl.multiple_of(owner_core * rows + h * half, half), half)]
+        start = (chip_at(oa, ob) * 2 + owner_core) * rows + h * half
+        return buf.at[pl.ds(pl.multiple_of(start, half), half)]
 
     sent = []
 
@@ -87,13 +88,12 @@
     for h in (0, 1):
         send(own(h), piece(0, 0, h, core), partner, 1, 0, 0, h)
     local = pltpu.make_async_copy(
-        x_ref, buf.at[chip_at(0, 0), pl.ds(pl.multiple_of(core * rows, rows), rows)], own_sem.at[0]
+        x_ref, buf.at[pl.ds(pl.multiple_of(me * rows, rows), rows)], own_sem.at[0]
     )
     local.start()
     local.wait()
     for h in (0, 1):
         arrived(1, 0, 0, h)
-    ready(chip_at(0, 0))
 
     arrived(0, 0, 1, 1)
     for o in others:
@@ -111,7 +111,6 @@
         relay(o, 0, 1)
     for h in (1, 0):
         arrived(1, 0, 1, h)
-    ready(chip_at(0, 1))
     for o in others:
         for h in (0, 1):
             arrived(0, o, 1, h)
@@ -119,11 +118,9 @@
     for o in others:
         for h in (0, 1):
             arrived(1, o, 0, h)
-        ready(chip_at(o, 0))
     for o in others:
         for h in (0, 1):
             arrived(1, o, 1, h)
-        ready(chip_at(o, 1))
     for copy in sent:
         copy.wait_send()
 
@@ -132,7 +129,7 @@
     a_size = tiles // 4
     copies = 2 + 2 * (a_size - 1) + 2 * (a_size - 1) + 2 * 2 * a_size
     return [
-        pltpu.VMEM((tiles // 2, 2 * shape[0]) + shape[1:], BF16),
+        pltpu.VMEM((tiles * shape[0],) + shape[1:], BF16),
         pltpu.SemaphoreType.DMA((copies,)),
         pltpu.SemaphoreType.DMA((2, 2 * a_size, 2)),
         pltpu.SemaphoreType.DMA((1,)),
@@ -140,17 +137,15 @@
 
 
 def pick_kernel(tiles, index_ref, x_ref, out_ref, buf, send_sem, recv_sem, own_sem):
-    gather_over_tile(tiles, x_ref, buf, send_sem, recv_sem, own_sem, lambda chip: None)
+    gather_over_tile(tiles, x_ref, buf, send_sem, recv_sem, own_sem)
     count = out_ref.shape[0]
-    pair = buf.shape[1]
-    step = 16
+    step = 32
 
     @pl.loop(0, count // step)
     def _(block):
         base = block * step
         for k in range(step):
-            index = index_ref[base + k]
-            out_ref[base + k] = buf[index // pair, lax.rem(index, pair)]
+            out_ref[base + k] = buf[index_ref[base + k]]
 
 
 def gather_and_pick(index, rows, tiles):
@@ -195,6 +190,9 @@
     half = share // 2
     lanes = width // 2
     blocks = rows // block
+    height = min(2 * block, rows)
+    each = height // block
+    steps = rows // height
     col = lax.axis_index("col")
     me = lax.axis_index("tile")
     core = lax.rem(me, 2)
@@ -220,21 +218,27 @@
     def at(i):
         return pl.ds(pl.multiple_of(i * block, block), block)
 
-    def fetch(i):
-        return pltpu.make_async_copy(z_ref.at[:, at(i)], z_buf.at[:, at(i)], z_sem.at[i])
-
-    @pl.loop(0, blocks)
+    def tall(t):
+        return pl.ds(pl.multiple_of(t * height, height), height)
+
+    def fetch(t):
+        return pltpu.make_async_copy(z_ref.at[:, tall(t)], z_buf.at[:, tall(t)], z_sem.at[t])
+
+    @pl.loop(0, steps)
     def _(i):
         fetch(i).start()
 
-    near = jnp.minimum(col, cols - 1 - col)
+    last = cols - 1
+    edge = jnp.logical_or(col == 0, col == last)
+    near = jnp.minimum(col, last - col)
 
     def group(k):
         side = col + (k + 1) // 2 if k % 2 else col - k // 2
-        rest = jnp.where(near == col, k, cols - 1 - k)
+        rest = jnp.where(near == col, k, last - k)
         return jnp.where(k <= 2 * near, side, rest)
 
-    order = [col] + [group(k) for k in range(1, cols)]
+    others_col = [group(k) for k in range(1, cols)]
+    order = [jnp.where(edge, a, b) for a, b in zip(others_col + [col], [col] + others_col)]
 
     def piece(g, oa, ob, h, owner_core):
         start = (chip_at(oa, ob) * 2 + owner_core) * share + h * half
@@ -246,18 +250,21 @@
 
     def swap(k):
         return pltpu.make_async_remote_copy(
-            src_ref=x_ref.at[order[k]],
+            src_ref=x_ref.at[others_col[k]],
             dst_ref=buf.at[col, own_rows],
-            send_sem=swap_send.at[k - 1],
+            send_sem=swap_send.at[k],
             recv_sem=swap_recv.at[col],
-            device_id={"col": order[k]},
+            device_id={"col": others_col[k]},
             device_id_type=MESH,
         )
 
-    for k in range(1, cols):
+    for k in range(last):
         swap(k).start()
-
-    sent = []
+    own = pltpu.make_async_copy(x_ref.at[col], buf.at[col, own_rows], own_sem.at[0])
+    own.start()
+    own.wait()
+
+    sends = [0]
 
     def gather(k):
         g = order[k]
@@ -266,13 +273,13 @@
             copy = pltpu.make_async_remote_copy(
                 src_ref=src,
                 dst_ref=dst,
-                send_sem=send_sem.at[len(sent)],
+                send_sem=send_sem.at[sends[0]],
                 recv_sem=recv_sem.at[k, relayed, oa * 2 + ob, h],
                 device_id={"tile": device},
                 device_id_type=MESH,
             )
             copy.start()
-            sent.append(copy)
+            sends[0] += 1
 
         def arrived(relayed, oa, ob, h):
             slot = piece(g, oa, ob, h, 1 - core if relayed else core)
@@ -293,20 +300,18 @@
             slot = piece(g, oa, ob, h, core)
             send(slot, slot, device, 0, new_oa, new_ob, h)
 
-        if k == 0:
-            local = pltpu.make_async_copy(x_ref.at[g], buf.at[g, own_rows], own_sem.at[0])
-            local.start()
-            local.wait()
-        else:
+        @pl.when(g != col)
+        def _():
             slot = buf.at[g, own_rows]
             pltpu.make_async_remote_copy(
                 src_ref=slot,
                 dst_ref=slot,
                 send_sem=swap_send.at[0],
                 recv_sem=swap_recv.at[g],
-                device_id={"col": g},
+                device_id={"col": lax.rem(col + 1, cols)},
                 device_id_type=MESH,
             ).wait_recv()
+
         for h in (1, 0):
             forward(0, 0, h, device_at(0, 1), 0, 1)
         for h in (0, 1):
@@ -346,9 +351,6 @@
                 arrived(1, o, 1, h)
         yield
 
-    last = cols - 1
-    edge = jnp.logical_or(col == 0, col == last)
-
     def pass_on(g, i):
         below = jnp.logical_and(g < col, g == col - 1)
         slot = jnp.where(below, cols, g)
@@ -371,47 +373,6 @@
             device_id_type=MESH,
         ).wait_recv()
 
-    def multiply(k, low, high):
-        g = order[k]
-
-        @pl.loop(low, high)
-        def _(i):
-            if k == 0:
-                fetch(i).wait()
-            x = buf[g]
-            a = jnp.dot(z_buf[0, at(i), :], x, preferred_element_type=F32)
-            b = jnp.dot(z_buf[1, at(i), :], x, preferred_element_type=F32)
-            term = jnp.concatenate([a[:, :lanes] - b[:, lanes:], a[:, lanes:] + b[:, :lanes]], 1)
-            if k == 0:
-                part[g, at(i), :] = term
-            else:
-
-                @pl.when(edge)
-                def _():
-                    sums[g, at(i), :] = term.astype(BF16)
-                    pass_on(g, i).start()
-
-                @pl.when(jnp.logical_not(edge))
-                def _():
-                    part[g, at(i), :] = term
-
-    stages = [gather(k) for k in range(cols)]
-    middle = blocks // 2
-    next(stages[0])
-    next(stages[0])
-    if cols > 1:
-        next(stages[1])
-    next(stages[0])
-    for k in range(cols):
-        multiply(k, 0, middle)
-        if k + 1 < cols:
-            next(stages[k + 1])
-        if k + 2 < cols:
-            next(stages[k + 2])
-        multiply(k, middle, blocks)
-        if k + 1 < cols:
-            next(stages[k + 1])
-
     lag = min(2, blocks)
     rising = 2 * col < cols
 
@@ -425,9 +386,63 @@
             sums[g, at(i), :] = (sums[g, at(i), :].astype(F32) + part[g, at(i), :]).astype(BF16)
             pass_on(g, i).start()
 
+    def multiply(k, midway):
+        g = order[k]
+        ends = jnp.logical_and(edge, g != col)
+
+        @pl.loop(0, steps)
+        def _(t):
+            @pl.when(t == steps // 2)
+            def _():
+                midway()
+
+            if k == 0:
+                fetch(t).wait()
+            at_t = tall(t)
+            x = buf[g]
+            a = jnp.dot(z_buf[0, at_t, :], x, preferred_element_type=F32)
+            b = jnp.dot(z_buf[1, at_t, :], x, preferred_element_type=F32)
+            term = jnp.concatenate([a[:, :lanes] - b[:, lanes:], a[:, lanes:] + b[:, :lanes]], 1)
+
+            @pl.when(ends)
+            def _():
+                sums[g, at_t, :] = term.astype(BF16)
+                for n in range(each):
+                    pass_on(g, t * each + n).start()
+
+            @pl.when(jnp.logical_not(ends))
+            def _():
+                part[g, at_t, :] = term
+
+            if k == last and cols > 2:
+
+                @pl.when(jnp.logical_not(edge))
+                def _():
+                    for n in range(each):
+                        flow(rising, 2, t * each + n)
+                        flow(jnp.logical_not(rising), 2, t * each + n)
+
+    stages = [gather(k) for k in range(cols)]
+    def advance(k):
+        if k < cols:
+            next(stages[k])
+
+    advance(0)
+    advance(0)
+    advance(1)
+    advance(0)
+    for k in range(cols):
+
+        def midway():
+            advance(k + 1)
+            advance(k + 2)
+
+        multiply(k, midway)
+        advance(k + 1)
+
     @pl.when(jnp.logical_not(edge))
     def _():
-        for turn in range(1, cols):
+        for turn in range(3, cols):
 
             @pl.loop(0, blocks + lag)
             def _(i):
@@ -453,16 +468,24 @@
 
         out_ref[at(i), :] = part[col, at(i), :].astype(BF16)
 
-    for k in range(1, cols):
+    for g in others_col:
 
         @pl.loop(0, blocks)
         def _(i):
-            pass_on(order[k], i).wait_send()
-
-    for k in range(1, cols):
+            pass_on(g, i).wait_send()
+
+    for k in range(last):
         swap(k).wait_send()
-    for copy in sent:
-        copy.wait_send()
+    for n in range(sends[0]):
+        slot = piece(0, 0, 0, 0, core)
+        pltpu.make_async_remote_copy(
+            src_ref=slot,
+            dst_ref=slot,
+            send_sem=send_sem.at[n],
+            recv_sem=recv_sem.at[0, 0, 0, 0],
+            device_id={"tile": partner},
+            device_id_type=MESH,
+        ).wait_send()
 
 
 def couple(impedance, x, tiles):
@@ -499,18 +522,20 @@
     )(impedance, x)
 
 
-def inverse_permutation(sigma):
+def places_of(sigma, tile, cols, tiles):
     count = sigma.shape[0]
+    per = count // cols // tiles // LANES
     where = jnp.arange(count, dtype=jnp.int32)
-    high = (sigma // LANES)[None, :] == jnp.arange(count // LANES, dtype=jnp.int32)[:, None]
-    low = (sigma % LANES)[:, None] == jnp.arange(LANES, dtype=jnp.int32)[None, :]
-    where_high = jnp.where(low, (where // LANES)[:, None], 0).astype(BF16)
-    where_low = jnp.where(low, (where % LANES)[:, None], 0).astype(BF16)
-    digits = jnp.dot(
-        high.astype(BF16), jnp.concatenate([where_high, where_low], 1), preferred_element_type=F32
-    )
-    inverse = digits[:, :LANES] * LANES + digits[:, LANES:]
-    return inverse.astype(jnp.int32).reshape(count)
+    col = jnp.arange(cols, dtype=jnp.int32)[:, None]
+    heads = ((col * tiles + tile) * per + jnp.arange(per, dtype=jnp.int32)[None, :]).reshape(-1)
+    high = (sigma // LANES)[None, :] == heads[:, None]
+    low = (sigma % LANES)[None, :] == jnp.arange(LANES, dtype=jnp.int32)[:, None]
+    digits = jnp.stack([where // LANES, where % LANES])
+    left = jnp.where(high[None], digits[:, None, :], 0).astype(BF16).reshape(-1, count)
+    found = lax.dot_general(
+        left, low.astype(BF16), (((1,), (1,)), ((), ())), preferred_element_type=F32
+    ).reshape(2, -1)
+    return (found[0] * LANES + found[1]).astype(jnp.int32)
 
 
 def per_device(impedance, mobility, force, patch_map, ownership):
@@ -526,32 +551,39 @@
     panels = patch_map.reshape(-1, width)
     slot_flat = panels[ownership].reshape(mine)
     owners = lax.all_gather(ownership, "tile", axis=0, tiled=True)
-    inverse = inverse_permutation(panels[owners].reshape(patches))
-    share_index = lax.dynamic_index_in_dim(
-        inverse.reshape(cols, tiles, share), tile, 1, keepdims=False
-    ).reshape(cols * share)
+    share_index = places_of(panels[owners].reshape(patches), tile, cols, tiles)
 
     mob_re = mobility[:, :, :width]
     mob_im = mobility[:, :, width:]
-    form = jnp.stack(
-        [jnp.stack([mob_re, -mob_im], -1), jnp.stack([mob_im, mob_re], -1)], 2
-    ).reshape(slots, 2 * width, 2 * width)
-    force_rows = force.reshape(loads, slots, 2, width).transpose(1, 3, 2, 0).reshape(slots, 2 * width, loads)
-
-    def response(drive):
-        return lax.dot_general(
-            form, drive, (((2,), (1,)), ((0,), (0,))), preferred_element_type=F32
-        ).astype(BF16)
-
-    velocity = response(force_rows)
-    for _ in range(ITERS):
+    plain = jnp.concatenate(
+        [jnp.concatenate([mob_re, -mob_im], 2), jnp.concatenate([mob_im, mob_re], 2)], 1
+    )
+    entry = jnp.arange(2 * width, dtype=jnp.int32)
+    mixed = (entry % 2) * width + entry // 2
+    mix = (mixed[:, None] == entry[None, :]).astype(BF16)
+
+    def product(a, a_dim, b, b_dim, a_batch=0, b_batch=0):
+        return lax.dot_general(a, b, (((a_dim,), (b_dim,)), ((a_batch,), (b_batch,))), preferred_element_type=F32)
+
+    def rows_mixed(a):
+        many = jnp.broadcast_to(mix, (slots,) + mix.shape)
+        return product(many, 2, a, 1).astype(BF16)
+
+    by_pair = lax.dot_general(plain, mix, (((2,), (1,)), ((), ())), preferred_element_type=F32).astype(BF16)
+    pair_force = rows_mixed(plain)
+    pair_pair = rows_mixed(by_pair)
+    first = product(pair_force, 2, force, 2, 0, 1)
+    first_out = product(force, 2, plain, 2, 1, 0)
+
+    velocity = first.astype(BF16)
+    for turn in range(ITERS):
         picked = gather_and_pick(share_index, velocity.reshape(mine, 2, loads), tiles)
         summed = couple(impedance, picked.reshape(cols, share, 2 * loads), tiles)
         pressure = summed.reshape(-1, 2, loads)
         at_slots = gather_and_pick(slot_flat, pressure, tiles).reshape(slots, 2 * width, loads)
-        drive = (force_rows.astype(F32) - at_slots.astype(F32)).astype(BF16)
-        velocity = response(drive)
-    velocity_out = velocity.reshape(slots, width, 2, loads).transpose(3, 0, 2, 1).reshape(loads, slots, 2 * width)
+        if turn < ITERS - 1:
+            velocity = (first - product(pair_pair, 2, at_slots, 1)).astype(BF16)
+    velocity_out = (first_out - product(at_slots, 1, by_pair, 2)).astype(BF16).transpose(1, 0, 2)
     pressure_out = pressure.transpose(2, 1, 0)
     return velocity_out, pressure_out
 

time: 508 us -> 440 us (0.87)
  Pallas kernels: 451 us -> 398 us
  local copies, waits for them, and re-layouts: 29.4 us -> 13.9 us
  matrix products: 3.54 us -> 13.3 us
  other arithmetic: 12.3 us -> 3.17 us
    pallas_call x4, Pallas kernels: 206 us -> 166 us  [gather_and_pick(): pl.pallas_call(functools.partial(pick_kernel, tiles), out_shape=jax.Shape...]
    pallas_call x2, Pallas kernels: 245 us -> 232 us  [couple(): pl.pallas_call(functools.partial(couple_kernel, tiles, cols, block), out_...]
    convert_element_type x6 -> x3, other arithmetic: 11 us -> 0.3 us  [the longest x1 0.21 us: places_of(): jnp.where(high[None], digits[:, None, :], 0).astype(BF16).reshape(-1, count)]
    dot_general x4 -> x6, matrix products: 3.54 us -> 13.3 us  [the longest x4 8.53 us: product(): lax.dot_general(a, b, (((a_dim,), (b_dim,)), ((a_batch,), (b_batch,))), p...]
    another operation x2 -> x0, local copies, waits for them, and re-layouts: 7.73 us -> none  [the longest x1 7.72 us: per_device(): jnp.stack([jnp.stack([mob_re, -mob_im], -1), jnp.stack([mob_im, mob_re],...]
where the time goes in v2:
time: 440 us; the launch traced here: 439 us
  Pallas kernels  398 us (90%)
  local copies, waits for them, and re-layouts  13.9 us (3%)
  matrix products  13.3 us (3%)
  blocking collectives  9.49 us (2%)
    pallas_call x2, Pallas kernels, couple(): pl.pallas_call(functools.partial(couple_kernel, tiles, cols, block), out_...  232 us
    pallas_call x4, Pallas kernels, gather_and_pick(): pl.pallas_call(functools.partial(pick_kernel, tiles), out_shape=jax.Shape...  166 us
    unnamed x1, blocking collectives  9.49 us

profile of v2, /device:TPU:0, one launch (start us, length us, event | category | flops | bytes accessed | tf_op | source)
XLA Modules:
  0.0 439.1 jit_solution(4501679468176893713)
XLA Ops:
  0.6 2.3 slice_negate_fusion
  3.0 0.1 fusion.12
  3.1 4.4 fusion.21
  7.6 0.6 dynamic-slice
  8.8 0.2 dynamic-update-slice
  9.1 9.5 %all-reduce = s32[256]{0:T(256)S(1)} all-reduce(s32[256]{0:T(256)S(1)} %dynamic-update-slice), channel_id=1, replica_groups=mesh['tile'=8,'col'=4] {'tile'}, use_global_device_ids=true, to_apply=%add | all-reduce | flops 256 | bytes 2048
  18.6 0.7 gather_fusion.1
  19.3 0.1 reshape.226
  19.6 0.1 add.120
  19.6 0.2 broadcast_compare_fusion
  19.9 0.1 and_select_fusion
  20.0 0.1 pad_add_fusion
  20.1 0.2 select_convert_fusion
  20.3 1.6 fusion
  21.9 41.1 %shard_map.68 = bf16[2048,2,128]{2,1,0:T(2,128)(2,1)S(1)} custom-call(s32[2048]{0:T(1024)S(1)} %fusion.18.index_ref, bf16[2048,2,128]{2,1,0:T(2,128)(2,1)S(1)} %bitcast.27), custom_call_target="tpu_custom_call" | custom-call | tf_op jit(solution)/shard_map/pallas_call | solution.py:152
  63.0 1.5 reshape.228.x_ref
  64.5 116.4 %shard_map.69 = bf16[2048,256]{1,0:T(8,128)(2,1)} custom-call(bf16[2,2048,4096]{2,1,0:T(8,128)(2,1)} %z_ref.3, bf16[4,512,256]{2,1,0:T(8,128)(2,1)} %reshape.228.x_ref), custom_call_target="tpu_custom_call" | custom-call | tf_op jit(solution)/shard_map/pallas_call | solution.py:497
  180.9 1.3 reshape.229.x_ref
  182.3 0.6 gather_fusion
  183.0 41.4 %shard_map.70 = bf16[2048,2,128]{2,1,0:T(2,128)(2,1)S(1)} custom-call(s32[2048]{0:T(1024)S(1)} %reshape.225.index_ref, bf16[2048,2,128]{2,1,0:T(2,128)(2,1)S(1)} %reshape.229.x_ref), custom_call_target="tpu_custom_call" | custom-call | tf_op jit(solution)/shard_map/pallas_call | solution.py:152
  224.4 3.2 convolution_convert_fusion.1
  227.6 2.7 subtract_convert_fusion
  230.3 41.9 %shard_map.71 = bf16[2048,2,128]{2,1,0:T(2,128)(2,1)S(1)} custom-call(s32[2048]{0:T(1024)S(1)} %fusion.18.index_ref, bf16[2048,2,128]{2,1,0:T(2,128)(2,1)S(1)} %bitcast.26), custom_call_target="tpu_custom_call" | custom-call | tf_op jit(solution)/shard_map/pallas_call | solution.py:152
  272.2 1.5 reshape.232.x_ref
  273.7 115.3 %shard_map.72 = bf16[2048,256]{1,0:T(8,128)(2,1)} custom-call(bf16[2,2048,4096]{2,1,0:T(8,128)(2,1)} %z_ref.3, bf16[4,512,256]{2,1,0:T(8,128)(2,1)} %reshape.232.x_ref), custom_call_target="tpu_custom_call" | custom-call | tf_op jit(solution)/shard_map/pallas_call | solution.py:497
  389.0 1.4 reshape.233.x_ref
  390.5 41.4 %shard_map.73 = bf16[2048,2,128]{2,1,0:T(2,128)(2,1)S(1)} custom-call(s32[2048]{0:T(1024)S(1)} %reshape.225.index_ref, bf16[2048,2,128]{2,1,0:T(2,128)(2,1)S(1)} %reshape.233.x_ref), custom_call_target="tpu_custom_call" | custom-call | tf_op jit(solution)/shard_map/pallas_call | solution.py:152
  432.0 1.0 fusion.5
  433.0 0.2 copy-done.1
  433.2 0.5 fusion.2
  433.7 1.7 copy.17
  435.4 3.7 copy.18
  (31 shorter events, 0.4 us)
Async XLA Ops:
  0.6 2.4 copy-start
  2.9 4.5 %copy-start.2 = (bf16[32,64,64]{2,1,0:T(8,128)(2,1)}, bf16[32,64,64]{2,1,0:T(8,128)(2,1)S(1)}, u32[]{:S(2)}) copy-start(bf16[32,64,64]{2,1,0:T(8,128)(2,1)S(1)} %get-tuple-element.6) | copy-start | bytes 786436
  2.9 4.5 %copy-start.4 = (bf16[32,64,64]{2,1,0:T(8,128)(2,1)}, bf16[32,64,64]{2,1,0:T(8,128)(2,1)S(1)}, u32[]{:S(2)}) copy-start(bf16[32,64,64]{2,1,0:T(8,128)(2,1)S(1)} %get-tuple-element.7) | copy-start | bytes 786436
  3.1 4.4 %copy-start.7 = (s32[16384]{0:T(1024)S(1)}, s32[16384]{0:T(1024)}, u32[]{:S(2)}) copy-start(s32[16384]{0:T(1024)} %param.8) | copy-start | bytes 196612
  3.1 4.5 %copy-start.9 = (u32[32]{0:T(128)S(1)}, u32[32]{0:T(128)}, u32[]{:S(2)}) copy-start(u32[32]{0:T(128)} %constant.91) | copy-start | bytes 388
  3.1 5.8 %copy-start.8 = (s32[32]{0:T(128)S(1)}, s32[32]{0:T(128)}, u32[]{:S(2)}) copy-start(s32[32]{0:T(128)} %param.9) | copy-start | bytes 388
  389.0 42.9 %copy-start.3 = (bf16[32,64,64]{2,1,0:T(8,128)(2,1)S(1)}, bf16[32,64,64]{2,1,0:T(8,128)(2,1)}, u32[]{:S(2)}) copy-start(bf16[32,64,64]{2,1,0:T(8,128)(2,1)} %copy-done.2) | copy-start | bytes 786436
  389.0 42.9 %copy-start.5 = (bf16[32,64,64]{2,1,0:T(8,128)(2,1)S(1)}, bf16[32,64,64]{2,1,0:T(8,128)(2,1)}, u32[]{:S(2)}) copy-start(bf16[32,64,64]{2,1,0:T(8,128)(2,1)} %copy-done.4) | copy-start | bytes 786436
  390.5 41.5 %copy-start.6 = (bf16[32,64,64]{2,1,0:T(8,128)(2,1)S(1)}, bf16[32,64,64]{2,1,0:T(8,128)(2,1)}, u32[]{:S(2)}) copy-start(bf16[32,64,64]{2,1,0:T(8,128)(2,1)} %get-tuple-element.8) | copy-start | bytes 786436
  432.0 1.2 copy-start.1

commit v3 on v2

--- a/solution.py
+++ b/solution.py
@@ -167,15 +167,17 @@
 def couple_kernel(
     tiles,
     cols,
-    block,
+    index_ref,
     z_ref,
     x_ref,
     out_ref,
+    own_ref,
     z_buf,
     z_sem,
     buf,
     part,
     sums,
+    whole,
     swap_send,
     swap_recv,
     own_sem,
@@ -185,14 +187,13 @@
     sum_recv,
 ):
     a_size = tiles // 4
-    rows, width = out_ref.shape
+    rows, _, lanes = own_ref.shape
     share = x_ref.shape[1]
-    half = share // 2
-    lanes = width // 2
+    height = rows // 4
+    each = 4
+    block = height // each
     blocks = rows // block
-    height = min(2 * block, rows)
-    each = height // block
-    steps = rows // height
+    slots = z_buf.shape[0]
     col = lax.axis_index("col")
     me = lax.axis_index("tile")
     core = lax.rem(me, 2)
@@ -222,14 +223,15 @@
         return pl.ds(pl.multiple_of(t * height, height), height)
 
     def fetch(t):
-        return pltpu.make_async_copy(z_ref.at[:, tall(t)], z_buf.at[:, tall(t)], z_sem.at[t])
-
-    @pl.loop(0, steps)
-    def _(i):
-        fetch(i).start()
+        slot = lax.rem(t, slots)
+        return pltpu.make_async_copy(z_ref.at[:, tall(t)], z_buf.at[slot], z_sem.at[t])
+
+    for t in range(3):
+        fetch(t).start()
 
     last = cols - 1
     edge = jnp.logical_or(col == 0, col == last)
+    inner = jnp.logical_not(edge)
     near = jnp.minimum(col, last - col)
 
     def group(k):
@@ -240,9 +242,11 @@
     others_col = [group(k) for k in range(1, cols)]
     order = [jnp.where(edge, a, b) for a, b in zip(others_col + [col], [col] + others_col)]
 
-    def piece(g, oa, ob, h, owner_core):
-        start = (chip_at(oa, ob) * 2 + owner_core) * share + h * half
-        return buf.at[g, pl.ds(pl.multiple_of(start, half), half)]
+    def order_at(k):
+        g = order[0]
+        for n in range(1, cols):
+            g = jnp.where(k == n, order[n], g)
+        return g
 
     own_rows = pl.ds(pl.multiple_of(me * share, share), share)
 
@@ -264,54 +268,39 @@
     own.start()
     own.wait()
 
-    sends = [0]
-
-    def gather(k):
-        g = order[k]
-
-        def send(src, dst, device, relayed, oa, ob, h):
-            copy = pltpu.make_async_remote_copy(
-                src_ref=src,
-                dst_ref=dst,
-                send_sem=send_sem.at[sends[0]],
-                recv_sem=recv_sem.at[k, relayed, oa * 2 + ob, h],
+    drains = []
+
+    def spread(turn, piece, before=None):
+        def send(slot, device, relayed, oa, ob, h):
+            pltpu.make_async_remote_copy(
+                src_ref=slot,
+                dst_ref=slot,
+                send_sem=send_sem.at[len(drains)],
+                recv_sem=recv_sem.at[turn, relayed, oa * 2 + ob, h],
                 device_id={"tile": device},
                 device_id_type=MESH,
-            )
-            copy.start()
-            sends[0] += 1
+            ).start()
+            drains.append(piece)
 
         def arrived(relayed, oa, ob, h):
-            slot = piece(g, oa, ob, h, 1 - core if relayed else core)
+            slot = piece(oa, ob, h, 1 - core if relayed else core)
             pltpu.make_async_remote_copy(
                 src_ref=slot,
                 dst_ref=slot,
                 send_sem=send_sem.at[0],
-                recv_sem=recv_sem.at[k, relayed, oa * 2 + ob, h],
+                recv_sem=recv_sem.at[turn, relayed, oa * 2 + ob, h],
                 device_id={"tile": partner},
                 device_id_type=MESH,
             ).wait_recv()
 
         def relay(oa, ob, h):
-            slot = piece(g, oa, ob, h, core)
-            send(slot, slot, partner, 1, oa, ob, h)
+            send(piece(oa, ob, h, core), partner, 1, oa, ob, h)
 
         def forward(oa, ob, h, device, new_oa, new_ob):
-            slot = piece(g, oa, ob, h, core)
-            send(slot, slot, device, 0, new_oa, new_ob, h)
-
-        @pl.when(g != col)
-        def _():
-            slot = buf.at[g, own_rows]
-            pltpu.make_async_remote_copy(
-                src_ref=slot,
-                dst_ref=slot,
-                send_sem=swap_send.at[0],
-                recv_sem=swap_recv.at[g],
-                device_id={"col": lax.rem(col + 1, cols)},
-                device_id_type=MESH,
-            ).wait_recv()
-
+            send(piece(oa, ob, h, core), device, 0, new_oa, new_ob, h)
+
+        if before is not None:
+            before()
         for h in (1, 0):
             forward(0, 0, h, device_at(0, 1), 0, 1)
         for h in (0, 1):
@@ -351,6 +340,38 @@
                 arrived(1, o, 1, h)
         yield
 
+    def gather(k):
+        g = order[k]
+        half = share // 2
+
+        def piece(oa, ob, h, owner_core):
+            start = (chip_at(oa, ob) * 2 + owner_core) * share + h * half
+            return buf.at[g, pl.ds(pl.multiple_of(start, half), half)]
+
+        def before():
+            @pl.when(g != col)
+            def _():
+                slot = buf.at[g, own_rows]
+                pltpu.make_async_remote_copy(
+                    src_ref=slot,
+                    dst_ref=slot,
+                    send_sem=swap_send.at[0],
+                    recv_sem=swap_recv.at[g],
+                    device_id={"col": lax.rem(col + 1, cols)},
+                    device_id_type=MESH,
+                ).wait_recv()
+
+        return spread(k, piece, before)
+
+    def share_part(p, low, high):
+        half = (high - low) * height // 2
+
+        def piece(oa, ob, h, owner_core):
+            start = (chip_at(oa, ob) * 2 + owner_core) * rows + low * height + h * half
+            return whole.at[pl.ds(pl.multiple_of(start, half), half)]
+
+        return spread(cols + p, piece)
+
     def pass_on(g, i):
         below = jnp.logical_and(g < col, g == col - 1)
         slot = jnp.where(below, cols, g)
@@ -373,7 +394,7 @@
             device_id_type=MESH,
         ).wait_recv()
 
-    lag = min(2, blocks)
+    lag = 2
     rising = 2 * col < cols
 
     def flow(up, turn, i):
@@ -386,43 +407,77 @@
             sums[g, at(i), :] = (sums[g, at(i), :].astype(F32) + part[g, at(i), :]).astype(BF16)
             pass_on(g, i).start()
 
-    def multiply(k, midway):
-        g = order[k]
+    def multiply(k, t):
+        g = order_at(k)
         ends = jnp.logical_and(edge, g != col)
 
-        @pl.loop(0, steps)
-        def _(t):
-            @pl.when(t == steps // 2)
+        @pl.when(k == 0)
+        def _():
+            fetch(t).wait()
+
+        slot = lax.rem(t, slots)
+        x = buf[g]
+        a = jnp.dot(z_buf[slot, 0], x, preferred_element_type=F32)
+        b = jnp.dot(z_buf[slot, 1], x, preferred_element_type=F32)
+        term = jnp.concatenate([a[:, :lanes] - b[:, lanes:], a[:, lanes:] + b[:, :lanes]], 1)
+
+        @pl.when(ends)
+        def _():
+            sums[g, tall(t), :] = term.astype(BF16)
+
+            @pl.loop(0, each)
+            def _(n):
+                pass_on(g, t * each + n).start()
+
+        @pl.when(jnp.logical_not(ends))
+        def _():
+            part[g, tall(t), :] = term
+
+        if cols > 2:
+
+            @pl.when(jnp.logical_and(inner, k == last))
             def _():
-                midway()
-
-            if k == 0:
-                fetch(t).wait()
-            at_t = tall(t)
-            x = buf[g]
-            a = jnp.dot(z_buf[0, at_t, :], x, preferred_element_type=F32)
-            b = jnp.dot(z_buf[1, at_t, :], x, preferred_element_type=F32)
-            term = jnp.concatenate([a[:, :lanes] - b[:, lanes:], a[:, lanes:] + b[:, :lanes]], 1)
-
-            @pl.when(ends)
+                @pl.loop(0, each)
+                def _(n):
+                    flow(rising, 2, t * each + n)
+                    flow(jnp.logical_not(rising), 2, t * each + n)
+
+    def forwards(low, high):
+        first, count = low * each, (high - low) * each
+
+        @pl.when(inner)
+        def _():
+            for turn in range(3, cols):
+
+                @pl.loop(0, count + lag)
+                def _(i):
+                    @pl.when(i < count)
+                    def _():
+                        flow(rising, turn, first + i)
+
+                    @pl.when(i >= lag)
+                    def _():
+                        flow(jnp.logical_not(rising), turn, first + i - lag)
+
+    def finish(low, high):
+        @pl.loop(low * each, high * each)
+        def _(i):
+            @pl.when(col > 0)
             def _():
-                sums[g, at_t, :] = term.astype(BF16)
-                for n in range(each):
-                    pass_on(g, t * each + n).start()
-
-            @pl.when(jnp.logical_not(ends))
+                passed(col, i)
+                part[col, at(i), :] += sums[col, at(i), :].astype(F32)
+
+            @pl.when(col < last)
             def _():
-                part[g, at_t, :] = term
-
-            if k == last and cols > 2:
-
-                @pl.when(jnp.logical_not(edge))
-                def _():
-                    for n in range(each):
-                        flow(rising, 2, t * each + n)
-                        flow(jnp.logical_not(rising), 2, t * each + n)
+                passed(cols, i)
+                part[col, at(i), :] += sums[cols, at(i), :].astype(F32)
+
+            total = part[col, at(i), :]
+            pair = jnp.stack([total[:, :lanes], total[:, lanes:]], 1).astype(BF16)
+            whole[pl.ds(pl.multiple_of(me * rows + i * block, block), block)] = pair
 
     stages = [gather(k) for k in range(cols)]
+
     def advance(k):
         if k < cols:
             next(stages[k])
@@ -431,43 +486,63 @@
     advance(0)
     advance(1)
     advance(0)
-    for k in range(cols):
-
-        def midway():
-            advance(k + 1)
-            advance(k + 2)
-
-        multiply(k, midway)
-        advance(k + 1)
-
-    @pl.when(jnp.logical_not(edge))
-    def _():
-        for turn in range(3, cols):
-
-            @pl.loop(0, blocks + lag)
-            def _(i):
-                @pl.when(i < blocks)
-                def _():
-                    flow(rising, turn, i)
-
-                @pl.when(i >= lag)
-                def _():
-                    flow(jnp.logical_not(rising), turn, i - lag)
-
-    @pl.loop(0, blocks)
-    def _(i):
-        @pl.when(col > 0)
-        def _():
-            passed(col, i)
-            part[col, at(i), :] += sums[col, at(i), :].astype(F32)
-
-        @pl.when(col < last)
-        def _():
-            passed(cols, i)
-            part[col, at(i), :] += sums[cols, at(i), :].astype(F32)
-
-        out_ref[at(i), :] = part[col, at(i), :].astype(BF16)
-
+
+    @pl.loop(0, 2 * cols)
+    def _(n):
+        for k in range(cols):
+
+            @pl.when(n == 2 * k + 1)
+            def _():
+                advance(k + 1)
+                advance(k + 2)
+
+            @pl.when(n == 2 * k + 2)
+            def _():
+                advance(k + 1)
+
+        multiply(n // 2, lax.rem(n, 2))
+
+    fetch(3).start()
+    parts = [share_part(0, 0, 2), share_part(1, 2, 3), share_part(2, 3, 4)]
+
+    forwards(0, 2)
+
+    @pl.loop(0, cols)
+    def _(k):
+        multiply(k, 2)
+
+    finish(0, 2)
+    next(parts[0])
+    forwards(2, 3)
+
+    @pl.loop(0, cols)
+    def _(k):
+        multiply(k, 3)
+
+    next(parts[0])
+    finish(2, 3)
+    next(parts[1])
+    next(parts[0])
+    forwards(3, 4)
+    finish(3, 4)
+    mine = pltpu.make_async_copy(
+        whole.at[pl.ds(pl.multiple_of(me * rows, rows), rows)], own_ref, own_sem.at[0]
+    )
+    mine.start()
+    next(parts[1])
+    next(parts[2])
+    next(parts[1])
+    next(parts[2])
+    next(parts[2])
+    step = 32
+
+    @pl.loop(0, out_ref.shape[0] // step)
+    def _(n):
+        base = n * step
+        for k in range(step):
+            out_ref[base + k] = whole[index_ref[base + k]]
+
+    mine.wait()
     for g in others_col:
 
         @pl.loop(0, blocks)
@@ -476,8 +551,8 @@
 
     for k in range(last):
         swap(k).wait_send()
-    for n in range(sends[0]):
-        slot = piece(0, 0, 0, 0, core)
+    for n, piece in enumerate(drains):
+        slot = piece(0, 0, 0, core)
         pltpu.make_async_remote_copy(
             src_ref=slot,
             dst_ref=slot,
@@ -488,38 +563,45 @@
         ).wait_send()
 
 
-def couple(impedance, x, tiles):
+def couple(index, impedance, x, tiles):
     _, rows, depth = impedance.shape
     cols, share, width = x.shape
     a_size = tiles // 4
-    block = min(256, rows)
-    copies = cols * (2 + 2 * (a_size - 1) + 2 * (a_size - 1) + 2 * 2 * a_size)
+    height = rows // 4
+    blocks = 16
+    lanes = width // 2
+    copies = (cols + 3) * (2 + 2 * (a_size - 1) + 2 * (a_size - 1) + 2 * 2 * a_size)
     return pl.pallas_call(
-        functools.partial(couple_kernel, tiles, cols, block),
-        out_shape=jax.ShapeDtypeStruct((rows, width), BF16),
+        functools.partial(couple_kernel, tiles, cols),
+        out_shape=(
+            jax.ShapeDtypeStruct((index.shape[0], 2, lanes), BF16),
+            jax.ShapeDtypeStruct((rows, 2, lanes), BF16),
+        ),
         in_specs=[
+            pl.BlockSpec(memory_space=pltpu.SMEM),
             pl.BlockSpec(memory_space=pl.ANY),
             pl.BlockSpec(memory_space=pltpu.VMEM),
         ],
-        out_specs=pl.BlockSpec(memory_space=pltpu.VMEM),
+        out_specs=(pl.BlockSpec(memory_space=pltpu.VMEM), pl.BlockSpec(memory_space=pltpu.VMEM)),
         scratch_shapes=[
-            pltpu.VMEM((2, rows, depth), BF16),
-            pltpu.SemaphoreType.DMA((rows // block,)),
+            pltpu.VMEM((3, 2, height, depth), BF16),
+            pltpu.SemaphoreType.DMA((4,)),
             pltpu.VMEM((cols, depth, width), BF16),
             pltpu.VMEM((cols, rows, width), F32),
             pltpu.VMEM((cols + 1, rows, width), BF16),
+            pltpu.VMEM((tiles * rows, 2, lanes), BF16),
             pltpu.SemaphoreType.DMA((max(cols - 1, 1),)),
             pltpu.SemaphoreType.DMA((cols,)),
             pltpu.SemaphoreType.DMA((1,)),
             pltpu.SemaphoreType.DMA((copies,)),
-            pltpu.SemaphoreType.DMA((cols, 2, 2 * a_size, 2)),
-            pltpu.SemaphoreType.DMA((cols, rows // block)),
-            pltpu.SemaphoreType.DMA((cols + 1, rows // block)),
+            pltpu.SemaphoreType.DMA((cols + 3, 2, 2 * a_size, 2)),
+            pltpu.SemaphoreType.DMA((cols, blocks)),
+            pltpu.SemaphoreType.DMA((cols + 1, blocks)),
         ],
         compiler_params=pltpu.CompilerParams(
             collective_id=1, has_side_effects=True, vmem_limit_bytes=60 * 2**20
         ),
-    )(impedance, x)
+    )(index, impedance, x)
 
 
 def places_of(sigma, tile, cols, tiles):
@@ -578,9 +660,8 @@
     velocity = first.astype(BF16)
     for turn in range(ITERS):
         picked = gather_and_pick(share_index, velocity.reshape(mine, 2, loads), tiles)
-        summed = couple(impedance, picked.reshape(cols, share, 2 * loads), tiles)
-        pressure = summed.reshape(-1, 2, loads)
-        at_slots = gather_and_pick(slot_flat, pressure, tiles).reshape(slots, 2 * width, loads)
+        at_slots, pressure = couple(slot_flat, impedance, picked.reshape(cols, share, 2 * loads), tiles)
+        at_slots = at_slots.reshape(slots, 2 * width, loads)
         if turn < ITERS - 1:
             velocity = (first - product(pair_pair, 2, at_slots, 1)).astype(BF16)
     velocity_out = (first_out - product(at_slots, 1, by_pair, 2)).astype(BF16).transpose(1, 0, 2)

time: 440 us -> 418 us (0.950)
  Pallas kernels: 398 us -> 380 us
    pallas_call x4 -> x2, Pallas kernels: 166 us -> 83.5 us  [gather_and_pick(): pl.pallas_call(functools.partial(pick_kernel, tiles), out_shape=jax.Shape...]
    pallas_call x2, Pallas kernels: 232 us -> 296 us  [couple(): pl.pallas_call(functools.partial(couple_kernel, tiles, cols), out_shape=(...]
where the time goes in v3:
time: 418 us; the launch traced here: 417 us
  Pallas kernels  380 us (91%)
  local copies, waits for them, and re-layouts  12.1 us (3%)
  matrix products  11.1 us (3%)
  blocking collectives  9.5 us (2%)
    pallas_call x2, Pallas kernels, couple(): pl.pallas_call(functools.partial(couple_kernel, tiles, cols), out_shape=(...  296 us
    pallas_call x2, Pallas kernels, gather_and_pick(): pl.pallas_call(functools.partial(pick_kernel, tiles), out_shape=jax.Shape...  83.5 us
    unnamed x1, blocking collectives  9.5 us
    dot_general x4, matrix products, product(): lax.dot_general(a, b, (((a_dim,), (b_dim,)), ((a_batch,), (b_batch,))), p...  8.84 us

profile of v3, /device:TPU:0, one launch (start us, length us, event | category | flops | bytes accessed | tf_op | source)
XLA Modules:
  0.0 417.2 jit_solution(16184835999014754776)
XLA Ops:
  0.6 2.3 slice_negate_fusion
  2.9 0.1 fusion.12
  3.1 4.4 %fusion.21 = (bf16[32,128,128]{2,1,0:T(8,128)(2,1)S(1)}, f32[32,128,128]{2,1,0:T(8,128)}) fusion(bf16[128,32,128]{2,1,0:T(8,128)(2,1)S(1)} %copy-done, bf16[128,128]{1,0:T(8,128)(2,1)S(1)} %fusion.12, bf16[32,64,64]{2,1,0:T(8,128)(2,1)} %get-tuple-element.14, bf16[32,64,64]{2,1,0:T(8,128)(2,1)S(1)} %get-tuple-element.13, ...), kind=kOutput, calls=%fused_computation.56 | convolution fusion | flops 273678336 | bytes 5013504 | tf_op jit(solution)/shard_map/dot_general | solution.py:648
  7.5 0.1 reshape.218
  7.6 0.6 dynamic-slice
  8.8 0.2 dynamic-update-slice
  9.1 9.5 %all-reduce = s32[256]{0:T(256)S(1)} all-reduce(s32[256]{0:T(256)S(1)} %dynamic-update-slice), channel_id=1, replica_groups=mesh['tile'=8,'col'=4] {'tile'}, use_global_device_ids=true, to_apply=%add | all-reduce | flops 256 | bytes 2048
  18.6 0.7 gather_fusion.1
  19.3 0.1 reshape.220
  19.5 0.1 iota_add_fusion
  19.6 0.1 add.120
  19.6 0.2 broadcast_compare_fusion
  19.9 0.1 and_select_fusion
  20.0 0.1 pad_add_fusion
  20.1 0.2 select_convert_fusion
  20.3 1.6 fusion
  21.9 41.1 %shard_map.68 = bf16[2048,2,128]{2,1,0:T(2,128)(2,1)S(1)} custom-call(s32[2048]{0:T(1024)S(1)} %fusion.18.index_ref, bf16[2048,2,128]{2,1,0:T(2,128)(2,1)S(1)} %bitcast.24), custom_call_target="tpu_custom_call" | custom-call | tf_op jit(solution)/shard_map/pallas_call | solution.py:152
  63.0 1.5 reshape.222.x_ref
  64.5 0.6 gather_fusion
  65.1 0.7 reshape.219.index_ref
  65.8 150.8 %shard_map.69 = (bf16[2048,2,128]{2,1,0:T(2,128)(2,1)}, bf16[2048,2,128]{2,1,0:T(2,128)(2,1)}) custom-call(s32[2048]{0:T(1024)} %reshape.219.index_ref, bf16[2,2048,4096]{2,1,0:T(8,128)(2,1)} %z_ref.3, bf16[4,512,256]{2,1,0:T(8,128)(2,1)} %reshape.222.x_ref), custom_call_target="tpu_custom_call" | custom-call | tf_op jit(solution)/shard_map/pallas_call | solution.py:574
  216.6 0.7 convolution_convert_fusion.1
  217.3 3.0 subtract_convert_fusion
  220.3 42.4 %shard_map.70 = bf16[2048,2,128]{2,1,0:T(2,128)(2,1)S(1)} custom-call(s32[2048]{0:T(1024)S(1)} %fusion.18.index_ref, bf16[2048,2,128]{2,1,0:T(2,128)(2,1)S(1)} %bitcast.23), custom_call_target="tpu_custom_call" | custom-call | tf_op jit(solution)/shard_map/pallas_call | solution.py:152
  262.7 1.5 reshape.225.x_ref
  264.2 145.5 %shard_map.71 = (bf16[2048,2,128]{2,1,0:T(2,128)(2,1)}, bf16[2048,2,128]{2,1,0:T(2,128)(2,1)}) custom-call(s32[2048]{0:T(1024)} %reshape.219.index_ref, bf16[2,2048,4096]{2,1,0:T(8,128)(2,1)} %z_ref.3, bf16[4,512,256]{2,1,0:T(8,128)(2,1)} %reshape.225.x_ref), custom_call_target="tpu_custom_call" | custom-call | tf_op jit(solution)/shard_map/pallas_call | solution.py:574
  409.8 1.0 fusion.5
  410.8 0.2 copy-done.2
  411.0 0.3 copy-done.3
  411.3 0.5 fusion.2
  411.8 1.7 copy.17
  413.5 3.7 copy.18
  (39 shorter events, 0.2 us)
Async XLA Ops:
  0.6 2.4 copy-start
  2.9 4.5 %copy-start.5 = (bf16[32,64,64]{2,1,0:T(8,128)(2,1)}, bf16[32,64,64]{2,1,0:T(8,128)(2,1)S(1)}, u32[]{:S(2)}) copy-start(bf16[32,64,64]{2,1,0:T(8,128)(2,1)S(1)} %get-tuple-element.12) | copy-start | bytes 786436
  2.9 4.5 %copy-start.8 = (bf16[32,64,64]{2,1,0:T(8,128)(2,1)}, bf16[32,64,64]{2,1,0:T(8,128)(2,1)S(1)}, u32[]{:S(2)}) copy-start(bf16[32,64,64]{2,1,0:T(8,128)(2,1)S(1)} %get-tuple-element.13) | copy-start | bytes 786436
  3.0 4.4 %copy-start.13 = (s32[16384]{0:T(1024)S(1)}, s32[16384]{0:T(1024)}, u32[]{:S(2)}) copy-start(s32[16384]{0:T(1024)} %param.8) | copy-start | bytes 196612
  3.0 4.5 %copy-start.15 = (u32[32]{0:T(128)S(1)}, u32[32]{0:T(128)}, u32[]{:S(2)}) copy-start(u32[32]{0:T(128)} %constant.91) | copy-start | bytes 388
  3.1 5.8 %copy-start.14 = (s32[32]{0:T(128)S(1)}, s32[32]{0:T(128)}, u32[]{:S(2)}) copy-start(s32[32]{0:T(128)} %param.9) | copy-start | bytes 388
  65.8 150.8 %copy-start.6 = (bf16[32,64,64]{2,1,0:T(8,128)(2,1)S(1)}, bf16[32,64,64]{2,1,0:T(8,128)(2,1)}, u32[]{:S(2)}) copy-start(bf16[32,64,64]{2,1,0:T(8,128)(2,1)} %copy-done.5) | copy-start | bytes 786436
  65.8 150.8 %copy-start.9 = (bf16[32,64,64]{2,1,0:T(8,128)(2,1)S(1)}, bf16[32,64,64]{2,1,0:T(8,128)(2,1)}, u32[]{:S(2)}) copy-start(bf16[32,64,64]{2,1,0:T(8,128)(2,1)} %copy-done.8) | copy-start | bytes 786436
  65.8 150.8 %copy-start.11 = (bf16[32,64,64]{2,1,0:T(8,128)(2,1)S(1)}, bf16[32,64,64]{2,1,0:T(8,128)(2,1)}, u32[]{:S(2)}) copy-start(bf16[32,64,64]{2,1,0:T(8,128)(2,1)} %get-tuple-element.14) | copy-start | bytes 786436
  217.3 3.0 copy-start.1
  264.2 145.5 %copy-start.7 = (bf16[32,64,64]{2,1,0:T(8,128)(2,1)S(1)}, bf16[32,64,64]{2,1,0:T(8,128)(2,1)}, u32[]{:S(2)}) copy-start(bf16[32,64,64]{2,1,0:T(8,128)(2,1)} %copy-done.5) | copy-start | bytes 786436
  264.2 145.6 %copy-start.10 = (bf16[32,64,64]{2,1,0:T(8,128)(2,1)S(1)}, bf16[32,64,64]{2,1,0:T(8,128)(2,1)}, u32[]{:S(2)}) copy-start(bf16[32,64,64]{2,1,0:T(8,128)(2,1)} %copy-done.8) | copy-start | bytes 786436
  264.2 145.6 %copy-start.12 = (bf16[32,64,64]{2,1,0:T(8,128)(2,1)S(1)}, bf16[32,64,64]{2,1,0:T(8,128)(2,1)}, u32[]{:S(2)}) copy-start(bf16[32,64,64]{2,1,0:T(8,128)(2,1)} %get-tuple-element.14) | copy-start | bytes 786436
  409.8 1.2 copy-start.2
  409.8 1.5 copy-start.3
  411.8 1.7 copy-start.4

commit v4 on v3

--- a/solution.py
+++ b/solution.py
@@ -407,7 +407,7 @@
             sums[g, at(i), :] = (sums[g, at(i), :].astype(F32) + part[g, at(i), :]).astype(BF16)
             pass_on(g, i).start()
 
-    def multiply(k, t):
+    def multiply(k, t, passing):
         g = order_at(k)
         ends = jnp.logical_and(edge, g != col)
 
@@ -433,7 +433,7 @@
         def _():
             part[g, tall(t), :] = term
 
-        if cols > 2:
+        if passing and cols > 2:
 
             @pl.when(jnp.logical_and(inner, k == last))
             def _():
@@ -442,12 +442,12 @@
                     flow(rising, 2, t * each + n)
                     flow(jnp.logical_not(rising), 2, t * each + n)
 
-    def forwards(low, high):
+    def forwards(turns, low, high):
         first, count = low * each, (high - low) * each
 
         @pl.when(inner)
         def _():
-            for turn in range(3, cols):
+            for turn in turns:
 
                 @pl.loop(0, count + lag)
                 def _(i):
@@ -500,36 +500,39 @@
             def _():
                 advance(k + 1)
 
-        multiply(n // 2, lax.rem(n, 2))
+        multiply(n // 2, lax.rem(n, 2), True)
 
     fetch(3).start()
     parts = [share_part(0, 0, 2), share_part(1, 2, 3), share_part(2, 3, 4)]
 
-    forwards(0, 2)
+    early, late = range(2, min(3, cols)), range(3, cols)
 
     @pl.loop(0, cols)
     def _(k):
-        multiply(k, 2)
-
+        multiply(k, 2, False)
+
+    forwards(late, 0, 2)
     finish(0, 2)
     next(parts[0])
-    forwards(2, 3)
 
     @pl.loop(0, cols)
     def _(k):
-        multiply(k, 3)
-
+        multiply(k, 3, False)
+
+    forwards(early, 2, 3)
     next(parts[0])
+    forwards(late, 2, 3)
     finish(2, 3)
     next(parts[1])
+    forwards(early, 3, 4)
     next(parts[0])
-    forwards(3, 4)
+    next(parts[1])
+    forwards(late, 3, 4)
     finish(3, 4)
     mine = pltpu.make_async_copy(
         whole.at[pl.ds(pl.multiple_of(me * rows, rows), rows)], own_ref, own_sem.at[0]
     )
     mine.start()
-    next(parts[1])
     next(parts[2])
     next(parts[1])
     next(parts[2])

time: 418 us -> 397 us (0.950)
  Pallas kernels: 380 us -> 359 us
    pallas_call x2, Pallas kernels: 296 us -> 274 us  [couple(): pl.pallas_call(functools.partial(couple_kernel, tiles, cols), out_shape=(...]
where the time goes in v4:
time: 397 us; the launch traced here: 396 us
  Pallas kernels  359 us (90%)
  local copies, waits for them, and re-layouts  12.1 us (3%)
  matrix products  11.1 us (3%)
  blocking collectives  9.5 us (2%)
    pallas_call x2, Pallas kernels, couple(): pl.pallas_call(functools.partial(couple_kernel, tiles, cols), out_shape=(...  274 us
    pallas_call x2, Pallas kernels, gather_and_pick(): pl.pallas_call(functools.partial(pick_kernel, tiles), out_shape=jax.Shape...  84.2 us
    unnamed x1, blocking collectives  9.5 us
    dot_general x4, matrix products, product(): lax.dot_general(a, b, (((a_dim,), (b_dim,)), ((a_batch,), (b_batch,))), p...  8.84 us

profile of v4, /device:TPU:0, one launch (start us, length us, event | category | flops | bytes accessed | tf_op | source)
XLA Modules:
  0.0 396.1 jit_solution(15748853781300326108)
XLA Ops:
  0.6 2.3 slice_negate_fusion
  2.9 0.1 fusion.12
  3.1 4.4 %fusion.21 = (bf16[32,128,128]{2,1,0:T(8,128)(2,1)S(1)}, f32[32,128,128]{2,1,0:T(8,128)}) fusion(bf16[128,32,128]{2,1,0:T(8,128)(2,1)S(1)} %copy-done, bf16[128,128]{1,0:T(8,128)(2,1)S(1)} %fusion.12, bf16[32,64,64]{2,1,0:T(8,128)(2,1)} %get-tuple-element.14, bf16[32,64,64]{2,1,0:T(8,128)(2,1)S(1)} %get-tuple-element.13, ...), kind=kOutput, calls=%fused_computation.56 | convolution fusion | flops 273678336 | bytes 5013504 | tf_op jit(solution)/shard_map/dot_general | solution.py:651
  7.5 0.1 reshape.218
  7.6 0.6 dynamic-slice
  8.8 0.2 dynamic-update-slice
  9.1 9.5 %all-reduce = s32[256]{0:T(256)S(1)} all-reduce(s32[256]{0:T(256)S(1)} %dynamic-update-slice), channel_id=1, replica_groups=mesh['tile'=8,'col'=4] {'tile'}, use_global_device_ids=true, to_apply=%add | all-reduce | flops 256 | bytes 2048
  18.6 0.7 gather_fusion.1
  19.3 0.1 reshape.220
  19.5 0.1 iota_add_fusion
  19.6 0.1 add.120
  19.6 0.2 broadcast_compare_fusion
  19.9 0.1 and_select_fusion
  20.0 0.1 pad_add_fusion
  20.1 0.2 select_convert_fusion
  20.3 1.6 fusion
  21.9 41.1 %shard_map.68 = bf16[2048,2,128]{2,1,0:T(2,128)(2,1)S(1)} custom-call(s32[2048]{0:T(1024)S(1)} %fusion.18.index_ref, bf16[2048,2,128]{2,1,0:T(2,128)(2,1)S(1)} %bitcast.24), custom_call_target="tpu_custom_call" | custom-call | tf_op jit(solution)/shard_map/pallas_call | solution.py:152
  63.0 1.5 reshape.222.x_ref
  64.5 0.6 gather_fusion
  65.1 0.7 reshape.219.index_ref
  65.8 138.6 %shard_map.69 = (bf16[2048,2,128]{2,1,0:T(2,128)(2,1)}, bf16[2048,2,128]{2,1,0:T(2,128)(2,1)}) custom-call(s32[2048]{0:T(1024)} %reshape.219.index_ref, bf16[2,2048,4096]{2,1,0:T(8,128)(2,1)} %z_ref.3, bf16[4,512,256]{2,1,0:T(8,128)(2,1)} %reshape.222.x_ref), custom_call_target="tpu_custom_call" | custom-call | tf_op jit(solution)/shard_map/pallas_call | solution.py:577
  204.4 0.7 convolution_convert_fusion.1
  205.1 3.0 subtract_convert_fusion
  208.2 43.1 %shard_map.70 = bf16[2048,2,128]{2,1,0:T(2,128)(2,1)S(1)} custom-call(s32[2048]{0:T(1024)S(1)} %fusion.18.index_ref, bf16[2048,2,128]{2,1,0:T(2,128)(2,1)S(1)} %bitcast.23), custom_call_target="tpu_custom_call" | custom-call | tf_op jit(solution)/shard_map/pallas_call | solution.py:152
  251.2 1.5 reshape.225.x_ref
  252.7 135.9 %shard_map.71 = (bf16[2048,2,128]{2,1,0:T(2,128)(2,1)}, bf16[2048,2,128]{2,1,0:T(2,128)(2,1)}) custom-call(s32[2048]{0:T(1024)} %reshape.219.index_ref, bf16[2,2048,4096]{2,1,0:T(8,128)(2,1)} %z_ref.3, bf16[4,512,256]{2,1,0:T(8,128)(2,1)} %reshape.225.x_ref), custom_call_target="tpu_custom_call" | custom-call | tf_op jit(solution)/shard_map/pallas_call | solution.py:577
  388.6 1.0 fusion.5
  389.6 0.2 copy-done.2
  389.9 0.3 copy-done.3
  390.2 0.5 fusion.2
  390.7 1.7 copy.17
  392.3 3.7 copy.18
  (39 shorter events, 0.2 us)
Async XLA Ops:
  0.6 2.4 copy-start
  2.9 4.5 %copy-start.5 = (bf16[32,64,64]{2,1,0:T(8,128)(2,1)}, bf16[32,64,64]{2,1,0:T(8,128)(2,1)S(1)}, u32[]{:S(2)}) copy-start(bf16[32,64,64]{2,1,0:T(8,128)(2,1)S(1)} %get-tuple-element.12) | copy-start | bytes 786436
  2.9 4.5 %copy-start.8 = (bf16[32,64,64]{2,1,0:T(8,128)(2,1)}, bf16[32,64,64]{2,1,0:T(8,128)(2,1)S(1)}, u32[]{:S(2)}) copy-start(bf16[32,64,64]{2,1,0:T(8,128)(2,1)S(1)} %get-tuple-element.13) | copy-start | bytes 786436
  3.0 4.4 %copy-start.13 = (s32[16384]{0:T(1024)S(1)}, s32[16384]{0:T(1024)}, u32[]{:S(2)}) copy-start(s32[16384]{0:T(1024)} %param.8) | copy-start | bytes 196612
  3.0 4.5 %copy-start.15 = (u32[32]{0:T(128)S(1)}, u32[32]{0:T(128)}, u32[]{:S(2)}) copy-start(u32[32]{0:T(128)} %constant.91) | copy-start | bytes 388
  3.1 5.8 %copy-start.14 = (s32[32]{0:T(128)S(1)}, s32[32]{0:T(128)}, u32[]{:S(2)}) copy-start(s32[32]{0:T(128)} %param.9) | copy-start | bytes 388
  65.8 138.6 %copy-start.6 = (bf16[32,64,64]{2,1,0:T(8,128)(2,1)S(1)}, bf16[32,64,64]{2,1,0:T(8,128)(2,1)}, u32[]{:S(2)}) copy-start(bf16[32,64,64]{2,1,0:T(8,128)(2,1)} %copy-done.5) | copy-start | bytes 786436
  65.8 138.6 %copy-start.9 = (bf16[32,64,64]{2,1,0:T(8,128)(2,1)S(1)}, bf16[32,64,64]{2,1,0:T(8,128)(2,1)}, u32[]{:S(2)}) copy-start(bf16[32,64,64]{2,1,0:T(8,128)(2,1)} %copy-done.8) | copy-start | bytes 786436
  65.8 138.6 %copy-start.11 = (bf16[32,64,64]{2,1,0:T(8,128)(2,1)S(1)}, bf16[32,64,64]{2,1,0:T(8,128)(2,1)}, u32[]{:S(2)}) copy-start(bf16[32,64,64]{2,1,0:T(8,128)(2,1)} %get-tuple-element.14) | copy-start | bytes 786436
  205.1 3.0 copy-start.1
  252.7 135.9 %copy-start.7 = (bf16[32,64,64]{2,1,0:T(8,128)(2,1)S(1)}, bf16[32,64,64]{2,1,0:T(8,128)(2,1)}, u32[]{:S(2)}) copy-start(bf16[32,64,64]{2,1,0:T(8,128)(2,1)} %copy-done.5) | copy-start | bytes 786436
  252.7 135.9 %copy-start.10 = (bf16[32,64,64]{2,1,0:T(8,128)(2,1)S(1)}, bf16[32,64,64]{2,1,0:T(8,128)(2,1)}, u32[]{:S(2)}) copy-start(bf16[32,64,64]{2,1,0:T(8,128)(2,1)} %copy-done.8) | copy-start | bytes 786436
  252.7 135.9 %copy-start.12 = (bf16[32,64,64]{2,1,0:T(8,128)(2,1)S(1)}, bf16[32,64,64]{2,1,0:T(8,128)(2,1)}, u32[]{:S(2)}) copy-start(bf16[32,64,64]{2,1,0:T(8,128)(2,1)} %get-tuple-element.14) | copy-start | bytes 786436
  388.6 1.2 copy-start.2
  388.6 1.5 copy-start.3
  390.6 1.7 copy-start.4
